TPU v7x, 512 devices: a whole 4x4x16 slice. The times are simulated.
512 devices in a mesh: src: 16 (over z_lo, core), tgt: 32 (over z_hi, y, x).
Axes of the slice: x: 4, y: 4, z: 16 (z_hi: 2, z_lo: 8; z = z_hi * 8 + z_lo), core: 2. Of those that a mesh axis runs over, the one named last changes fastest.
Arguments:
- src_feats: bfloat16 [32, 40960], P(None, ('src', 'tgt')), may hold values from -7 to 7
- src_factor: bfloat16 [16, 40960], P(None, ('src', 'tgt')), may hold values from 0.1 to 8
- tgt_feats: bfloat16 [32, 65536], P(None, ('tgt', 'src')), may hold values from -7 to 7
- tgt_factor: bfloat16 [16, 65536], P(None, ('tgt', 'src')), may hold values from 0.1 to 8
- rank_weight: float32 [16], replicated, may hold values from 0.5 to 4
Outputs:
- grad_src_feats: float32 [32, 40960], P(None, ('src', 'tgt'))
- grad_src_factor: float32 [16, 40960], P(None, ('src', 'tgt'))
- grad_tgt_feats: float32 [32, 65536], P(None, ('tgt', 'src'))
- grad_tgt_factor: float32 [16, 65536], P(None, ('tgt', 'src'))
All inputs are finite; a program needn't handle non-finite values.
Results may differ from a plain program's by a relative error of at most 0.0015.
Values may be sent and summed in bfloat16 or wider, within the bound.
No kernel may reach another device: no remote copies, remote signals or barrier semaphores. Data moves between devices by JAX's collectives and lax.ppermute only.
A program may use at most 64 MiB of HBM per device.

v0:
```python
import jax
import jax.numpy as jnp
from jax import lax
from jax.sharding import PartitionSpec as P


def tile_terms(src_x, src_q, tgt_y, scaled_r, inverse_g):
    sq_src = jnp.sum(jnp.square(src_x.astype(jnp.float32)), 0)
    sq_tgt = jnp.sum(jnp.square(tgt_y.astype(jnp.float32)), 0)
    inner_prod = jnp.dot(src_x.T, tgt_y, preferred_element_type=jnp.float32)
    distance = jnp.sqrt(sq_src[:, None] + sq_tgt[None, :] - 2.0 * inner_prod + 1.0)
    plan_tile = jnp.dot(src_q.T, scaled_r, preferred_element_type=jnp.float32)
    weight = (plan_tile / distance).astype(jnp.bfloat16)
    cost_bf = distance.astype(jnp.bfloat16)
    row_mass = jnp.sum(weight.astype(jnp.float32), 1)
    col_mass = jnp.sum(weight.astype(jnp.float32), 0)
    grad_x = src_x.astype(jnp.float32) * row_mass[None, :] - jnp.dot(
        tgt_y, weight.T, preferred_element_type=jnp.float32
    )
    grad_q = jnp.dot(scaled_r, cost_bf.T, preferred_element_type=jnp.float32)
    grad_y = tgt_y.astype(jnp.float32) * col_mass[None, :] - jnp.dot(
        src_x, weight, preferred_element_type=jnp.float32
    )
    grad_r = inverse_g[:, None] * jnp.dot(src_q, cost_bf, preferred_element_type=jnp.float32)
    return (jnp.concatenate([grad_x, grad_q], 0), jnp.concatenate([grad_y, grad_r], 0))


def block_size(count):
    for candidate in (512, 256, 128):
        return candidate
    return count


def local(src_feats, src_factor, tgt_feats, tgt_factor, rank_weight):
    feature_count = src_feats.shape[0]
    stacked_count = feature_count + src_factor.shape[0]
    inverse_g = 1.0 / rank_weight
    tgt_whole = lax.all_gather(
        jnp.concatenate([tgt_feats, tgt_factor], 0), "src", axis=1, tiled=True
    )
    tgt_points = tgt_whole[:feature_count]
    scaled_r = (tgt_whole[feature_count:].astype(jnp.float32) * inverse_g[:, None]).astype(
        jnp.bfloat16
    )
    col_count = tgt_points.shape[1]
    total_tgt = tgt_feats.shape[1] * lax.axis_size("src") * lax.axis_size("tgt")
    src_stack = jnp.concatenate([src_feats, src_factor], 0)
    src_whole = lax.all_gather(src_stack, "tgt", axis=1, tiled=True)
    row_count = src_whole.shape[1]
    block_rows = block_size(row_count)

    def advance(block_index, totals):
        src_acc, tgt_acc = totals
        offset = block_index * block_rows
        part = lax.dynamic_slice_in_dim(src_whole, offset, block_rows, 1)
        src_part, tgt_part = tile_terms(
            part[:feature_count], part[feature_count:], tgt_points, scaled_r, inverse_g
        )
        src_acc = lax.dynamic_update_slice_in_dim(src_acc, src_part, offset, 1)
        tgt_acc = tgt_acc + tgt_part
        return (src_acc, tgt_acc)

    src_start = jnp.zeros((stacked_count, row_count), jnp.float32)
    tgt_start = jnp.zeros((stacked_count, col_count), jnp.float32)
    src_terms, tgt_terms = lax.fori_loop(
        0, row_count // block_rows, advance, (src_start, tgt_start)
    )
    src_sum = lax.psum_scatter(src_terms, "tgt", scatter_dimension=1, tiled=True)
    tgt_sum = lax.psum_scatter(tgt_terms, "src", scatter_dimension=1, tiled=True)
    scale = 1.0 / total_tgt
    return (
        src_sum[:feature_count] * scale,
        src_sum[feature_count:] * scale,
        tgt_sum[:feature_count] * scale,
        tgt_sum[feature_count:] * scale,
    )


def solution(mesh):
    placed = (
        P(None, ("src", "tgt")),
        P(None, ("src", "tgt")),
        P(None, ("tgt", "src")),
        P(None, ("tgt", "src")),
        P(),
    )
    return jax.shard_map(
        local,
        mesh=mesh,
        in_specs=placed,
        out_specs=(
            P(None, ("src", "tgt")),
            P(None, ("src", "tgt")),
            P(None, ("tgt", "src")),
            P(None, ("tgt", "src")),
        ),
        check_vma=False,
    )
```

profile of v0, /device:TPU:32, one launch (start us, length us, event | category | flops | bytes accessed | tf_op | source)
XLA Modules:
  0.0 646.9 jit_solution(10596549005930550365)
XLA Ops:
  7.2 0.7 broadcast_divide_fusion
  7.9 0.7 pad_maximum_fusion
  8.6 31.1 %all_gather.7 = bf16[48,2048]{1,0:T(8,128)(2,1)S(1)} all-gather(bf16[48,128]{1,0:T(8,128)(2,1)S(1)} %pad_maximum_fusion), channel_id=1, replica_groups=mesh['src'=16,'tgt'=32] {'src'}, dimensions={1}, use_global_device_ids=true | all-gather | bytes 208896 | tf_op jit(solution)/shard_map/all_gather | solution.py:38
  39.8 0.7 maximum_bitcast_fusion
  40.5 160.2 %all-gather = bf16[32,80,48]{1,2,0:T(8,128)(2,1)S(1)} all-gather(bf16[1,80,48]{1,2,0:T(8,128)(2,1)S(1)} %maximum_bitcast_fusion), channel_id=1, replica_groups=mesh['src'=16,'tgt'=32] {'tgt'}, dimensions={0}, use_global_device_ids=true | all-gather | bytes 253440 | tf_op jit(solution)/shard_map/all_gather | solution.py:48
  200.8 0.6 reshape.15
  201.4 29.4 %while.16 = (s32[]{:T(128)}, f32[48,2560]{1,0:T(8,128)S(1)}, f32[48,2048]{1,0:T(8,128)S(1)}, bf16[48,2560]{1,0:T(8,128)(2,1)S(1)}, bf16[16,2048]{1,0:T(8,128)(2,...) while((s32[]{:T(128)}, f32[48,2560]{1,0:T(8,128)S(1)}, ...), condition=%wide.region_5.0_spmd.clone, body=%wide.region_0.0_spmd.clone.sunk | while | flops 314362880 | bytes 25797348 | solution.py:65
  201.5 2.3 add_sqrt_fusion.2
  203.9 0.6 convolution_bitcast_fusion.3
  204.5 0.4 convolution_multiply_fusion.2
  204.9 1.0 convert_reduce_fusion.3
  206.0 0.7 fusion.44
  206.7 0.5 convolution_subtract_fusion.2
  207.4 2.3 add_sqrt_fusion.2
  209.8 0.6 convolution_bitcast_fusion.3
  210.4 0.4 convolution_multiply_fusion.2
  210.8 1.0 convert_reduce_fusion.3
  211.8 0.7 fusion.44
  212.6 0.5 convolution_subtract_fusion.2
  213.3 2.3 add_sqrt_fusion.2
  215.6 0.6 convolution_bitcast_fusion.3
  216.3 0.4 convolution_multiply_fusion.2
  216.7 1.0 convert_reduce_fusion.3
  217.7 0.7 fusion.44
  218.4 0.5 convolution_subtract_fusion.2
  218.9 0.1 maximum_add_fusion.2
  219.2 2.3 add_sqrt_fusion.2
  221.5 0.6 convolution_bitcast_fusion.3
  222.2 0.4 convolution_multiply_fusion.2
  222.6 1.0 convert_reduce_fusion.3
  223.6 0.7 fusion.44
  224.3 0.5 convolution_subtract_fusion.2
  225.1 2.3 add_sqrt_fusion.2
  227.4 0.6 convolution_bitcast_fusion.3
  228.0 0.4 convolution_multiply_fusion.2
  228.5 1.0 convert_reduce_fusion.3
  229.5 0.7 fusion.44
  230.2 0.5 convolution_subtract_fusion.2
  230.9 0.7 copy-done
  231.7 1.5 copy.11
  233.2 88.0 %reduce-scatter.5.cloned.1.call-done = f32[48,128]{1,0:T(8,128)} async-done(((f32[48,2048]{1,0:T(8,128)}), f32[48,128]{1,0:T(8,128)}) %reduce-scatter.5.cloned.1.call-update) | async-done | bytes 24592 | tf_op jit(solution)/shard_map/reduce_scatter | solution.py:69
  321.2 1.3 slice_multiply_fusion.1
  322.5 1.3 slice_multiply_fusion
  323.8 313.2 %reduce-scatter.7.cloned.1.call-done = f32[80,48]{1,0:T(8,128)} async-done(((f32[2560,48]{1,0:T(8,128)}), f32[80,48]{1,0:T(8,128)}) %reduce-scatter.7.cloned.1.call-update) | async-done | bytes 15376
  637.0 0.9 slice.43
  637.9 0.8 copy.13
  638.7 0.6 broadcast_multiply_fusion
  639.4 0.6 broadcast_multiply_fusion.1
  (30 shorter events, 1.4 us)
Async XLA Ops:
  7.2 314.0 %reduce-scatter.5.cloned.1.call-start = ((), (), s32[]{:S(2)}) async-start(), calls=%async_computation.2 | async-start | bytes 417792 | tf_op jit(solution)/shard_map/reduce_scatter | solution.py:69
  230.8 0.8 copy-start
  231.6 405.4 %reduce-scatter.7.cloned.1.call-start = ((), (), s32[]{:S(2)}) async-start(), calls=%async_computation.3 | async-start | bytes 1351680
Sparse Core Ops, SparseCore 0:
  231.7 89.3 reduce-scatter.4
  324.2 312.7 reduce-scatter.6
where the time goes:
time: 647 us
  waiting for transfers between devices  401 us (62%)
  blocking collectives  191 us (30%)
  matrix products  28 us (4%)
  between operations  14.1 us (2%)
  other arithmetic  7.12 us (1%)
    unnamed x3, waiting for transfers between devices  313 us
    all_gather x1, blocking collectives, local(): src_whole = lax.all_gather(src_stack, 'tgt', axis=1, tiled=True)  160 us
    reduce_scatter x1, waiting for transfers between devices, local(): lax.psum_scatter(tgt_terms, 'src', scatter_dimension=1, tiled=True)  88 us
    all_gather x1, blocking collectives, local(): lax.all_gather(jnp.concatenate([tgt_feats, tgt_factor], 0), 'src', axis=1...  31.1 us
  transfers between devices with their start and end apart: 2, of which 2 were waited for; matrix products, arithmetic and copies ran while one was open for 1% of the time, Pallas kernels for 0%

commit v1 on v0

v1 whole, which is shorter than its diff:
```python
import jax
import jax.numpy as jnp
from jax import lax
from jax.sharding import Mesh
from jax.sharding import PartitionSpec as P

RING = ("zh", "zl")
PLANE = ("y", "x", "core")


def tile_terms(src_x, src_q, tgt_y, scaled_r, inverse_g):
    sq_src = jnp.sum(jnp.square(src_x.astype(jnp.float32)), 0)
    sq_tgt = jnp.sum(jnp.square(tgt_y.astype(jnp.float32)), 0)
    inner_prod = jnp.dot(src_x.T, tgt_y, preferred_element_type=jnp.float32)
    distance = jnp.sqrt(sq_src[:, None] + sq_tgt[None, :] - 2.0 * inner_prod + 1.0)
    plan_tile = jnp.dot(src_q.T, scaled_r, preferred_element_type=jnp.float32)
    weight = (plan_tile / distance).astype(jnp.bfloat16)
    cost_bf = distance.astype(jnp.bfloat16)
    row_mass = jnp.sum(weight.astype(jnp.float32), 1)
    col_mass = jnp.sum(weight.astype(jnp.float32), 0)
    grad_x = src_x.astype(jnp.float32) * row_mass[None, :] - jnp.dot(
        tgt_y, weight.T, preferred_element_type=jnp.float32
    )
    grad_q = jnp.dot(scaled_r, cost_bf.T, preferred_element_type=jnp.float32)
    grad_y = tgt_y.astype(jnp.float32) * col_mass[None, :] - jnp.dot(
        src_x, weight, preferred_element_type=jnp.float32
    )
    grad_r = inverse_g[:, None] * jnp.dot(src_q, cost_bf, preferred_element_type=jnp.float32)
    return (jnp.concatenate([grad_x, grad_q], 0), jnp.concatenate([grad_y, grad_r], 0))


def gather_blocks(block, axes):
    count = lax.axis_size(axes)
    copies = jnp.broadcast_to(block[None], (count, *block.shape))
    return lax.all_to_all(copies, axes, 0, 0, tiled=True)


def join(blocks):
    count, rows, cols = blocks.shape
    return jnp.transpose(blocks, (1, 0, 2)).reshape(rows, count * cols)


def reduce_blocks(whole, axes):
    count = lax.axis_size(axes)
    rows, cols = whole.shape
    parts = jnp.transpose(whole.reshape(rows, count, cols // count), (1, 0, 2))
    return jnp.sum(lax.all_to_all(parts, axes, 0, 0, tiled=True), 0)


def local(src_feats, src_factor, tgt_feats, tgt_factor, rank_weight):
    features = src_feats.shape[0]
    inverse_g = 1.0 / rank_weight
    total_tgt = tgt_feats.shape[1] * lax.axis_size(RING) * lax.axis_size(PLANE)
    src_whole = join(gather_blocks(jnp.concatenate([src_feats, src_factor], 0), PLANE))
    tgt_whole = join(gather_blocks(jnp.concatenate([tgt_feats, tgt_factor], 0), RING))
    tgt_points = tgt_whole[:features]
    scaled_r = (tgt_whole[features:].astype(jnp.float32) * inverse_g[:, None]).astype(
        jnp.bfloat16
    )
    rows = src_whole.shape[0]
    row_count = src_whole.shape[1]
    col_count = tgt_points.shape[1]
    block_rows = 512

    def advance(block_index, totals):
        src_acc, tgt_acc = totals
        offset = block_index * block_rows
        part = lax.dynamic_slice_in_dim(src_whole, offset, block_rows, 1)
        src_part, tgt_part = tile_terms(
            part[:features], part[features:], tgt_points, scaled_r, inverse_g
        )
        src_acc = lax.dynamic_update_slice_in_dim(src_acc, src_part, offset, 1)
        return (src_acc, tgt_acc + tgt_part)

    src_start = jnp.zeros((rows, row_count), jnp.float32)
    tgt_start = jnp.zeros((rows, col_count), jnp.float32)
    src_terms, tgt_terms = lax.fori_loop(
        0, row_count // block_rows, advance, (src_start, tgt_start)
    )
    tgt_sum = reduce_blocks(tgt_terms, RING)
    src_sum = reduce_blocks(src_terms, PLANE)
    scale = 1.0 / total_tgt
    return (
        src_sum[:features] * scale,
        src_sum[features:] * scale,
        tgt_sum[:features] * scale,
        tgt_sum[features:] * scale,
    )


def solution(mesh):
    fine = Mesh(mesh.devices.reshape(8, 2, 2, 4, 4), ("zl", "core", "zh", "y", "x"))
    src_axes = ("zl", "core", "zh", "y", "x")
    tgt_axes = ("zh", "y", "x", "zl", "core")
    by_src = P(None, src_axes)
    by_tgt = P(None, tgt_axes)
    return jax.shard_map(
        local,
        mesh=fine,
        in_specs=(by_src, by_src, by_tgt, by_tgt, P()),
        out_specs=(by_src, by_src, by_tgt, by_tgt),
        check_vma=False,
    )
```

time: 647 us -> 133 us (0.21)
  the two profiles are of different devices: /device:TPU:32 before, /device:TPU:6 now
where the time goes in v1:
time: 133 us
  waiting for transfers between devices  58.8 us (44%)
  starting transfers between devices  34.3 us (26%)
  matrix products  28 us (21%)
  other arithmetic  5.8 us (4%)
  local copies, waits for them, and re-layouts  4.91 us (4%)
    all_to_all x2, waiting for transfers between devices, reduce_blocks(): return jnp.sum(lax.all_to_all(parts, axes, 0, 0, tiled=True), 0)  36.6 us
    all_to_all x2, starting transfers between devices, gather_blocks(): return lax.all_to_all(copies, axes, 0, 0, tiled=True)  22.7 us
    all_to_all x2, waiting for transfers between devices, gather_blocks(): return lax.all_to_all(copies, axes, 0, 0, tiled=True)  22.3 us
    dot_general x5, matrix products, tile_terms(): inner_prod = jnp.dot(src_x.T, tgt_y, preferred_element_type=jnp.float32)  11.6 us
    all_to_all x2, starting transfers between devices, reduce_blocks(): return jnp.sum(lax.all_to_all(parts, axes, 0, 0, tiled=True), 0)  11.6 us
    dot_general x5, matrix products, tile_terms(): plan_tile = jnp.dot(src_q.T, scaled_r, preferred_element_type=jnp.float32)  5.11 us
    dot_general x5, matrix products, tile_terms(): jnp.dot(tgt_y, weight.T, preferred_element_type=jnp.float32)  3.65 us
    dot_general x5, matrix products, tile_terms(): grad_q = jnp.dot(scaled_r, cost_bf.T, preferred_element_type=jnp.float32)  3.22 us
  transfers between devices with their start and end apart: 4, of which 4 were waited for; matrix products, arithmetic and copies ran while one was open for 3% of the time, Pallas kernels for 0%

profile of v1, /device:TPU:6, one launch (start us, length us, event | category | flops | bytes accessed | tf_op | source)
XLA Modules:
  0.0 132.8 jit_solution(18145053536195231983)
XLA Ops:
  0.6 0.7 pad_maximum_fusion
  1.4 0.8 broadcast_in_dim.36
  2.1 9.4 %all-to-all-start = ((bf16[32,48,80]{2,1,0:T(8,128)(2,1)}), bf16[32,48,80]{2,1,0:T(8,128)(2,1)S(1)}, u32[]{:S(2)}, u32[]{:S(2)}) async-start(bf16[32,48,80]{2,1,0:T(8,128)(2,1)} %broadcast_in_dim.36), calls=%async_computation | async-start | bytes 786432 | tf_op jit(solution)/shard_map/all_to_all | solution.py:35
  11.6 0.7 pad_maximum_fusion.1
  12.3 7.4 %all-to-all-done = bf16[32,48,80]{2,1,0:T(8,128)(2,1)S(1)} async-done(((bf16[32,48,80]{2,1,0:T(8,128)(2,1)}), bf16[32,48,80]{2,1,0:T(8,128)(2,1)S(1)}, u32[]{:S(2)}, u32[]{:S(2)}) %all-to-all-start) | async-done | bytes 245792 | tf_op jit(solution)/shard_map/all_to_all | solution.py:35
  19.7 0.7 broadcast_in_dim.37
  20.4 13.3 %all-to-all-start.1 = ((bf16[16,48,128]{2,1,0:T(8,128)(2,1)}), bf16[16,48,128]{2,1,0:T(8,128)(2,1)S(1)}, u32[]{:S(2)}, u32[]{:S(2)}) async-start(bf16[16,48,128]{2,1,0:T(8,128)(2,1)} %broadcast_in_dim.37), calls=%async_computation.1 | async-start | bytes 393216 | tf_op jit(solution)/shard_map/all_to_all | solution.py:35
  33.7 0.7 broadcast_divide_fusion
  34.4 0.6 reshape.30
  35.0 14.9 %all-to-all-done.1 = bf16[16,48,128]{2,1,0:T(8,128)(2,1)S(1)} async-done(((bf16[16,48,128]{2,1,0:T(8,128)(2,1)}), bf16[16,48,128]{2,1,0:T(8,128)(2,1)S(1)}, u32[]{:S(2)}, u32[]{:S(2)}) %all-to-all-start.1) | async-done | bytes 196640 | tf_op jit(solution)/shard_map/all_to_all | solution.py:35
  50.0 29.4 %while.16 = (s32[]{:T(128)}, f32[48,2560]{1,0:T(8,128)S(1)}, f32[48,2048]{1,0:T(8,128)S(1)}, bf16[48,2560]{1,0:T(8,128)(2,1)S(1)}, bf16[16,2048]{1,0:T(8,128)(2,...) while((s32[]{:T(128)}, f32[48,2560]{1,0:T(8,128)S(1)}, ...), condition=%wide.region_5.0_spmd.clone, body=%wide.region_0.0_spmd.clone.sunk | while | flops 314362880 | bytes 25797348 | solution.py:77
  50.1 2.3 %add_sqrt_fusion.2 = f32[512,2048]{1,0:T(8,128)S(1)} fusion(bf16[32,2048]{1,0:T(8,128)(2,1)S(1)} %get-tuple-element.250, f32[2048]{0:T(1024)S(1)} %fusion.43, f32[512]{0:T(512)S(1)} %fusion.44, bf16[48,2560]{1,0:T(8,128)(2,1)S(1)} %get-tuple-element.248, s32[]{:T(128)S(6)} %select_n.10), kind=kOutput, calls=%fused_computation.3.clone.1 | convolution fusion | flops 71303168 | bytes 4368388 | tf_op jit(solution)/shard_map/while/body/eval_jaxpr/dot_general | solution.py:14
  52.5 0.6 convolution_bitcast_fusion.3
  53.1 0.4 convolution_multiply_fusion.2
  53.5 1.0 convert_reduce_fusion.3
  54.5 0.7 fusion.45
  55.3 0.5 convolution_subtract_fusion.2
  56.0 2.3 %add_sqrt_fusion.2 = f32[512,2048]{1,0:T(8,128)S(1)} fusion(bf16[32,2048]{1,0:T(8,128)(2,1)S(1)} %get-tuple-element.250, f32[2048]{0:T(1024)S(1)} %fusion.43, f32[512]{0:T(512)S(1)} %fusion.44, bf16[48,2560]{1,0:T(8,128)(2,1)S(1)} %get-tuple-element.248, s32[]{:T(128)S(6)} %select_n.10), kind=kOutput, calls=%fused_computation.3.clone.1 | convolution fusion | flops 71303168 | bytes 4368388 | tf_op jit(solution)/shard_map/while/body/eval_jaxpr/dot_general | solution.py:14
  58.3 0.6 convolution_bitcast_fusion.3
  59.4 1.0 convert_reduce_fusion.3
  60.4 0.7 fusion.45
  61.1 0.5 convolution_subtract_fusion.2
  61.9 2.3 %add_sqrt_fusion.2 = f32[512,2048]{1,0:T(8,128)S(1)} fusion(bf16[32,2048]{1,0:T(8,128)(2,1)S(1)} %get-tuple-element.250, f32[2048]{0:T(1024)S(1)} %fusion.43, f32[512]{0:T(512)S(1)} %fusion.44, bf16[48,2560]{1,0:T(8,128)(2,1)S(1)} %get-tuple-element.248, s32[]{:T(128)S(6)} %select_n.10), kind=kOutput, calls=%fused_computation.3.clone.1 | convolution fusion | flops 71303168 | bytes 4368388 | tf_op jit(solution)/shard_map/while/body/eval_jaxpr/dot_general | solution.py:14
  64.2 0.6 convolution_bitcast_fusion.3
  65.3 1.0 convert_reduce_fusion.3
  66.3 0.7 fusion.45
  67.0 0.5 convolution_subtract_fusion.2
  67.8 2.3 %add_sqrt_fusion.2 = f32[512,2048]{1,0:T(8,128)S(1)} fusion(bf16[32,2048]{1,0:T(8,128)(2,1)S(1)} %get-tuple-element.250, f32[2048]{0:T(1024)S(1)} %fusion.43, f32[512]{0:T(512)S(1)} %fusion.44, bf16[48,2560]{1,0:T(8,128)(2,1)S(1)} %get-tuple-element.248, s32[]{:T(128)S(6)} %select_n.10), kind=kOutput, calls=%fused_computation.3.clone.1 | convolution fusion | flops 71303168 | bytes 4368388 | tf_op jit(solution)/shard_map/while/body/eval_jaxpr/dot_general | solution.py:14
  70.1 0.6 convolution_bitcast_fusion.3
  71.1 1.0 convert_reduce_fusion.3
  72.2 0.7 fusion.45
  72.9 0.5 convolution_subtract_fusion.2
  73.6 2.3 %add_sqrt_fusion.2 = f32[512,2048]{1,0:T(8,128)S(1)} fusion(bf16[32,2048]{1,0:T(8,128)(2,1)S(1)} %get-tuple-element.250, f32[2048]{0:T(1024)S(1)} %fusion.43, f32[512]{0:T(512)S(1)} %fusion.44, bf16[48,2560]{1,0:T(8,128)(2,1)S(1)} %get-tuple-element.248, s32[]{:T(128)S(6)} %select_n.10), kind=kOutput, calls=%fused_computation.3.clone.1 | convolution fusion | flops 71303168 | bytes 4368388 | tf_op jit(solution)/shard_map/while/body/eval_jaxpr/dot_general | solution.py:14
  76.0 0.6 convolution_bitcast_fusion.3
  77.0 1.0 convert_reduce_fusion.3
  78.0 0.7 fusion.45
  78.8 0.5 convolution_subtract_fusion.2
  79.4 0.4 reshape.31
  79.8 1.3 %copy.12 = f32[32,48,80]{2,1,0:T(8,128)} copy(f32[32,48,80]{2,0,1:T(8,128)S(1)} %bitcast.48) | data formatting | bytes 983040 | tf_op jit(solution)/shard_map/transpose | solution.py:46
  81.2 6.2 %all-to-all-start.2 = ((f32[32,48,80]{2,1,0:T(8,128)}), f32[32,48,80]{2,1,0:T(8,128)S(1)}, u32[]{:S(2)}, u32[]{:S(2)}) async-start(f32[32,48,80]{2,1,0:T(8,128)} %copy.12), calls=%async_computation.2 | async-start | bytes 1572864 | tf_op jit(solution)/shard_map/all_to_all | solution.py:47
  87.4 0.9 copy.13
  88.3 11.0 %all-to-all-done.2 = f32[32,48,80]{2,1,0:T(8,128)S(1)} async-done(((f32[32,48,80]{2,1,0:T(8,128)}), f32[32,48,80]{2,1,0:T(8,128)S(1)}, u32[]{:S(2)}, u32[]{:S(2)}) %all-to-all-start.2) | async-done | bytes 491552 | tf_op jit(solution)/shard_map/all_to_all | solution.py:47
  99.3 5.4 %all-to-all-start.3 = ((f32[16,48,128]{2,1,0:T(8,128)}), f32[16,48,128]{2,1,0:T(8,128)S(1)}, u32[]{:S(2)}, u32[]{:S(2)}) async-start(f32[16,48,128]{2,1,0:T(8,128)} %copy.13), calls=%async_computation.3 | async-start | bytes 786432 | tf_op jit(solution)/shard_map/all_to_all | solution.py:47
  104.9 0.6 slice_multiply_fusion.3
  105.5 0.6 slice_multiply_fusion.1
  106.1 25.5 %all-to-all-done.3 = f32[16,48,128]{2,1,0:T(8,128)S(1)} async-done(((f32[16,48,128]{2,1,0:T(8,128)}), f32[16,48,128]{2,1,0:T(8,128)S(1)}, u32[]{:S(2)}, u32[]{:S(2)}) %all-to-all-start.3) | async-done | bytes 393248 | tf_op jit(solution)/shard_map/all_to_all | solution.py:47
  131.6 0.6 slice_multiply_fusion.2
  132.2 0.6 slice_multiply_fusion
  (32 shorter events, 3.1 us)
Async XLA Ops:
  2.1 17.5 %all-to-all-start = ((bf16[32,48,80]{2,1,0:T(8,128)(2,1)}), bf16[32,48,80]{2,1,0:T(8,128)(2,1)S(1)}, u32[]{:S(2)}, u32[]{:S(2)}) async-start(bf16[32,48,80]{2,1,0:T(8,128)(2,1)} %broadcast_in_dim.36), calls=%async_computation | async-start | bytes 786432 | tf_op jit(solution)/shard_map/all_to_all | solution.py:35
  20.4 29.5 %all-to-all-start.1 = ((bf16[16,48,128]{2,1,0:T(8,128)(2,1)}), bf16[16,48,128]{2,1,0:T(8,128)(2,1)S(1)}, u32[]{:S(2)}, u32[]{:S(2)}) async-start(bf16[16,48,128]{2,1,0:T(8,128)(2,1)} %broadcast_in_dim.37), calls=%async_computation.1 | async-start | bytes 393216 | tf_op jit(solution)/shard_map/all_to_all | solution.py:35
  81.2 18.2 %all-to-all-start.2 = ((f32[32,48,80]{2,1,0:T(8,128)}), f32[32,48,80]{2,1,0:T(8,128)S(1)}, u32[]{:S(2)}, u32[]{:S(2)}) async-start(f32[32,48,80]{2,1,0:T(8,128)} %copy.12), calls=%async_computation.2 | async-start | bytes 1572864 | tf_op jit(solution)/shard_map/all_to_all | solution.py:47
  99.3 32.2 %all-to-all-start.3 = ((f32[16,48,128]{2,1,0:T(8,128)}), f32[16,48,128]{2,1,0:T(8,128)S(1)}, u32[]{:S(2)}, u32[]{:S(2)}) async-start(f32[16,48,128]{2,1,0:T(8,128)} %copy.13), calls=%async_computation.3 | async-start | bytes 786432 | tf_op jit(solution)/shard_map/all_to_all | solution.py:47

commit v2 on v1

v2 whole, which is shorter than its diff:
```python
import jax
import jax.numpy as jnp
from jax import lax
from jax.experimental import pallas as pl
from jax.experimental.pallas import tpu as pltpu
from jax.sharding import Mesh
from jax.sharding import PartitionSpec as P

RING = ("zh", "zl")
PLANE = ("y", "x", "core")
BF16 = jnp.bfloat16
F32 = jnp.float32
VMEM = pl.BlockSpec(memory_space=pltpu.VMEM)
SMEM = pl.BlockSpec(memory_space=pltpu.SMEM)
STEP = 256


def dot(a, b):
    return jnp.dot(a, b, preferred_element_type=F32)


def inverse_column(rank_ref, width):
    rank = rank_ref.shape[0]
    rows = lax.broadcasted_iota(jnp.int32, (rank, width), 0)
    column = jnp.full((rank, width), rank_ref[0], F32)
    for k in range(1, rank):
        column = jnp.where(rows == k, rank_ref[k], column)
    return 1.0 / column


def copies_kernel(feats_ref, factor_ref, out_ref):
    block = jnp.concatenate([feats_ref[...], factor_ref[...]], 0)
    for member in range(out_ref.shape[0]):
        out_ref[member] = block


def scaled_copies_kernel(rank_ref, feats_ref, factor_ref, out_ref):
    factor = factor_ref[...]
    inverse_g = inverse_column(rank_ref, factor.shape[1])
    scaled = (factor.astype(F32) * inverse_g).astype(BF16)
    block = jnp.concatenate([feats_ref[...], scaled], 0)
    for member in range(out_ref.shape[0]):
        out_ref[member] = block


def three_parts(value):
    high = value.astype(BF16)
    rest = value - high.astype(F32)
    mid = rest.astype(BF16)
    low = (rest - mid.astype(F32)).astype(BF16)
    return [high.astype(F32), mid.astype(F32), low.astype(F32)]


def squares(feats):
    return jnp.sum(jnp.square(feats), 0, keepdims=True)


def pair_kernel(features, scale, is_target, rank_ref, lane_ref, sub_ref, out_ref, a_ref, gw_ref, gc_ref, bd_ref, bp_ref, x_ref, sum_ref):
    lane_blocks, rows, lane_width = lane_ref.shape
    sub_blocks, _, sub_width = sub_ref.shape
    rank = rows - features
    for b in range(sub_blocks):
        block = sub_ref[b].astype(F32)
        x = block[:features]
        q = block[features:]
        ones = jnp.ones((1, sub_width), F32)
        stack = jnp.concatenate(
            [-2.0 * x, q] + three_parts(squares(x)) + [ones] * 3 + [jnp.zeros((10, sub_width), F32)], 0
        )
        at = pl.ds(b * sub_width, sub_width)
        a_ref[at, :] = stack.T.astype(BF16)
        gw_ref[:, at] = jnp.concatenate([x, ones, jnp.zeros((7, sub_width), F32)], 0)
        gc_ref[:, at] = q
    for b in range(lane_blocks):
        x_ref[:, pl.ds(b * lane_width, lane_width)] = lane_ref[b].astype(F32)
    lanes = x_ref.shape[1]
    subs = a_ref.shape[0]
    for start in range(0, lanes, STEP):
        at = pl.ds(start, STEP)
        block = x_ref[:, at]
        x = block[:features]
        ones = jnp.ones((3, STEP), F32)
        tail = jnp.zeros((10, STEP), F32)
        bd_ref[:, at] = jnp.concatenate(
            [x, jnp.zeros((rank, STEP), F32), ones] + three_parts(squares(x) + 1.0) + [tail], 0
        ).astype(BF16)
        bp_ref[:, at] = jnp.concatenate(
            [jnp.zeros((features, STEP), F32), block[features:], jnp.zeros((16, STEP), F32)], 0
        ).astype(BF16)
    gw = gw_ref[...].astype(BF16)
    gc = gc_ref[...].astype(BF16)
    if is_target:
        factor_scale = inverse_column(rank_ref, STEP) * scale
    else:
        factor_scale = scale

    def advance(index, carry):
        at = pl.ds(pl.multiple_of(index * STEP, STEP), STEP)
        bd = bd_ref[:, at]
        bp = bp_ref[:, at]
        sum_w = jnp.zeros((gw.shape[0], STEP), F32)
        sum_c = jnp.zeros((rank, STEP), F32)
        for u in range(0, subs, STEP):
            a = a_ref[pl.ds(u, STEP), :]
            s = dot(a, bd)
            p = dot(a, bp)
            r = lax.rsqrt(s)
            w = (p * r).astype(BF16)
            c = (s * r).astype(BF16)
            sum_w += dot(gw[:, u : u + STEP], w)
            sum_c += dot(gc[:, u : u + STEP], c)
        x = x_ref[:, at][:features]
        grad = (x * sum_w[features : features + 1] - sum_w[:features]) * scale
        both = jnp.concatenate([grad, sum_c * factor_scale], 0)
        if is_target:
            per = STEP // lane_width
            for k in range(per):
                out_ref[index * per + k] = both[:, k * lane_width : (k + 1) * lane_width]
        else:
            sum_ref[:, at] = both
        return carry

    lax.fori_loop(0, lanes // STEP, advance, 0)
    if not is_target:
        half = lane_width // 2
        for b in range(lane_blocks):
            block = sum_ref[:, b * lane_width : (b + 1) * lane_width]
            factor = block[features:]
            out_ref[b] = jnp.concatenate(
                [
                    block[:features],
                    jnp.concatenate([factor[:, :half], factor[:, half:]], 0),
                    jnp.zeros((features, 128 - lane_width - half), F32),
                ],
                1,
            )


def target_sum_kernel(features, parts_ref, feats_ref, factor_ref):
    total = jnp.sum(parts_ref[...], 0)
    feats_ref[...] = total[:features]
    factor_ref[...] = total[features:]


def source_sum_kernel(rank, parts_ref, feats_ref, factor_ref):
    total = jnp.sum(parts_ref[...], 0)
    width = feats_ref.shape[1]
    half = width // 2
    feats_ref[...] = total[:, :width]
    factor_ref[:, :half] = total[:rank, width : width + half]
    factor_ref[:, half:] = total[rank:, width : width + half]


def call(kernel, specs, outs, scratch=(), flops=0):
    single = not isinstance(outs, tuple)
    return pl.pallas_call(
        kernel,
        out_shape=outs,
        in_specs=specs,
        out_specs=VMEM if single else tuple(VMEM for _ in outs),
        scratch_shapes=scratch,
        compiler_params=pltpu.CompilerParams(vmem_limit_bytes=40 << 20),
        cost_estimate=pl.CostEstimate(flops=flops, transcendentals=0, bytes_accessed=1 << 20),
    )


def exchange(blocks, axes):
    return lax.all_to_all(blocks, axes, 0, 0, tiled=True)


def local(src_feats, src_factor, tgt_feats, tgt_factor, rank_weight):
    features, src_width = src_feats.shape
    rank = src_factor.shape[0]
    rows = features + rank
    tgt_width = tgt_feats.shape[1]
    ring = lax.axis_size(RING)
    plane = lax.axis_size(PLANE)
    scale = 1.0 / (tgt_width * ring * plane)
    sources = ring * src_width
    targets = plane * tgt_width

    def shape(*dims, dtype=F32):
        return jax.ShapeDtypeStruct(dims, dtype)

    tgt_copies = call(scaled_copies_kernel, (SMEM, VMEM, VMEM), shape(plane, rows, tgt_width, dtype=BF16))(
        rank_weight, tgt_feats, tgt_factor
    )
    src_copies = call(copies_kernel, (VMEM, VMEM), shape(ring, rows, src_width, dtype=BF16))(
        src_feats, src_factor
    )
    tgt_blocks = exchange(tgt_copies, PLANE)
    src_blocks = exchange(src_copies, RING)

    def pairs(is_target, lane_blocks, sub_blocks, out):
        lanes = lane_blocks.shape[0] * lane_blocks.shape[2]
        subs = sub_blocks.shape[0] * sub_blocks.shape[2]
        scratch = (
            pltpu.VMEM((subs, 64), BF16),
            pltpu.VMEM((features + 8, subs), F32),
            pltpu.VMEM((rank, subs), F32),
            pltpu.VMEM((64, lanes), BF16),
            pltpu.VMEM((64, lanes), BF16),
            pltpu.VMEM((rows, lanes), F32),
            pltpu.VMEM((rows, lanes), F32),
        )

        def kernel(*refs):
            pair_kernel(features, scale, is_target, *refs)

        return call(kernel, (SMEM, VMEM, VMEM), out, scratch, flops=lanes * subs * 2 * 256 * 4)(
            rank_weight, lane_blocks, sub_blocks
        )

    tgt_parts = pairs(True, tgt_blocks, src_blocks, shape(plane, rows, tgt_width))
    tgt_parts = exchange(tgt_parts, PLANE)
    src_parts = pairs(False, src_blocks, tgt_blocks, shape(ring, features, 128))
    src_parts = exchange(src_parts, RING)

    def tgt_final(*refs):
        target_sum_kernel(features, *refs)

    def src_final(*refs):
        source_sum_kernel(rank, *refs)

    grad_y, grad_r = call(tgt_final, (VMEM,), (shape(features, tgt_width), shape(rank, tgt_width)))(tgt_parts)
    grad_x, grad_q = call(src_final, (VMEM,), (shape(features, src_width), shape(rank, src_width)))(src_parts)
    return grad_x, grad_q, grad_y, grad_r


def solution(mesh):
    fine = Mesh(mesh.devices.reshape(8, 2, 2, 4, 4), ("zl", "core", "zh", "y", "x"))
    by_src = P(None, ("zl", "core", "zh", "y", "x"))
    by_tgt = P(None, ("zh", "y", "x", "zl", "core"))
    return jax.shard_map(
        local,
        mesh=fine,
        in_specs=(by_src, by_src, by_tgt, by_tgt, P()),
        out_specs=(by_src, by_src, by_tgt, by_tgt),
        check_vma=False,
    )
```

time: 133 us -> 120 us (0.902)
  the two profiles are of different devices: /device:TPU:6 before, /device:TPU:2 now
where the time goes in v2:
time: 120 us; the launch traced here: 119 us
  Pallas kernels  40.3 us (34%)
  blocking collectives  28.9 us (24%)
  waiting for transfers between devices  27 us (22%)
  starting transfers between devices  20.5 us (17%)
  local copies, waits for them, and re-layouts  2.04 us (2%)
    pallas_call x2, Pallas kernels, pairs(): call(kernel, (SMEM, VMEM, VMEM), out, scratch, flops=lanes * subs * 2 * 2...  37.6 us
    all_to_all x1, blocking collectives, exchange(): return lax.all_to_all(blocks, axes, 0, 0, tiled=True)  28.9 us
    all_to_all x3, waiting for transfers between devices, exchange(): return lax.all_to_all(blocks, axes, 0, 0, tiled=True)  27 us
    all_to_all x3, starting transfers between devices, exchange(): return lax.all_to_all(blocks, axes, 0, 0, tiled=True)  20.5 us
  transfers between devices with their start and end apart: 3, of which 2 were waited for; matrix products, arithmetic and copies ran while one was open for 0% of the time, Pallas kernels for 16%

profile of v2, /device:TPU:2, one launch (start us, length us, event | category | flops | bytes accessed | tf_op | source)
XLA Modules:
  0.0 119.4 jit_solution(10855857798741664665)
XLA Ops:
  0.6 0.0 copy-start
  0.6 0.7 copy-done
  1.3 0.0 copy-start.2
  1.3 0.7 copy-done.2
  2.0 0.0 copy-start.4
  2.0 0.7 copy-done.4
  2.7 1.3 %shard_map.85 = bf16[32,48,128]{2,1,0:T(8,128)(2,1)} custom-call(f32[16]{0:T(128)S(1)} %copy-done.4, bf16[32,128]{1,0:T(8,128)(2,1)S(1)} %copy-done, bf16[16,128]{1,0:T(8,128)(2,1)S(1)} %copy-done.2), custom_call_target="tpu_custom_call" | custom-call | bytes 1048576 | tf_op jit(solution)/shard_map/pallas_call | solution.py:185
  4.0 0.0 copy-start.1
  4.0 0.0 copy-start.3
  4.0 9.6 %all-to-all-start.1 = ((bf16[32,48,128]{2,1,0:T(8,128)(2,1)}), bf16[32,48,128]{2,1,0:T(8,128)(2,1)S(1)}, u32[]{:S(2)}, u32[]{:S(2)}) async-start(bf16[32,48,128]{2,1,0:T(8,128)(2,1)} %shard_map.85), calls=%async_computation.1 | async-start | bytes 786432 | tf_op jit(solution)/shard_map/all_to_all | solution.py:168
  13.6 0.0 copy-done.1
  13.6 0.0 copy-done.3
  13.6 0.0 copy-start.5
  13.7 9.1 %all-to-all-done.1.refs_2_.refs_1_ = bf16[32,48,128]{2,1,0:T(8,128)(2,1)S(1)} async-done(((bf16[32,48,128]{2,1,0:T(8,128)(2,1)}), bf16[32,48,128]{2,1,0:T(8,128)(2,1)S(1)}, u32[]{:S(2)}, u32[]{:S(2)}) %all-to-all-start.1) | async-done | bytes 393248 | tf_op jit(solution)/shard_map/all_to_all | solution.py:168
  22.8 28.9 %all_to_all.20.refs_1_.refs_2_ = bf16[16,48,80]{2,1,0:T(8,128)(2,1)S(1)} all-to-all(bf16[16,48,80]{2,1,0:T(8,128)(2,1)S(1)} %shard_map.84), channel_id=1, replica_groups=mesh['zl'=8,'core'=2,'zh'=2,'y'=4,'x'=4] {'zh','zl'}, dimensions={0} | all-to-all | bytes 245760 | tf_op jit(solution)/shard_map/all_to_all | solution.py:168
  51.7 0.0 copy-done.5
  51.7 19.0 %shard_map.88 = f32[32,48,128]{2,1,0:T(8,128)} custom-call(f32[16]{0:T(128)S(1)} %copy-done.5, bf16[32,48,128]{2,1,0:T(8,128)(2,1)S(1)} %all-to-all-done.1.refs_2_.refs_1_, bf16[16,48,80]{2,1,0:T(8,128)(2,1)S(1)} %all_to_all.20.refs_1_.refs_2_), custom_call_target="tpu_custom_call" | custom-call | flops 10737418240 | bytes 1048576 | tf_op jit(solution)/shard_map/pallas_call | solution.py:210
  70.7 5.5 %all-to-all-start.3 = ((f32[32,48,128]{2,1,0:T(8,128)}), f32[32,48,128]{2,1,0:T(8,128)S(1)}, u32[]{:S(2)}, u32[]{:S(2)}) async-start(f32[32,48,128]{2,1,0:T(8,128)} %shard_map.88), calls=%async_computation.3 | async-start | bytes 1572864 | tf_op jit(solution)/shard_map/all_to_all | solution.py:168
  76.2 18.6 %shard_map.86 = f32[16,32,128]{2,1,0:T(8,128)} custom-call(f32[16]{0:T(128)S(1)} %copy-done.5, bf16[16,48,80]{2,1,0:T(8,128)(2,1)S(1)} %all_to_all.20.refs_1_.refs_2_, bf16[32,48,128]{2,1,0:T(8,128)(2,1)S(1)} %all-to-all-done.1.refs_2_.refs_1_), custom_call_target="tpu_custom_call" | custom-call | flops 10737418240 | bytes 1048576 | tf_op jit(solution)/shard_map/pallas_call | solution.py:210
  94.8 0.0 all-to-all-done.3.refs_0_
  94.8 5.4 %all-to-all-start.2 = ((f32[16,32,128]{2,1,0:T(8,128)}), f32[16,32,128]{2,1,0:T(8,128)S(1)}, u32[]{:S(2)}, u32[]{:S(2)}) async-start(f32[16,32,128]{2,1,0:T(8,128)} %shard_map.86), calls=%async_computation.2 | async-start | bytes 524288 | tf_op jit(solution)/shard_map/all_to_all | solution.py:168
  100.2 0.7 shard_map.89
  100.9 17.9 %all-to-all-done.2.refs_0_ = f32[16,32,128]{2,1,0:T(8,128)S(1)} async-done(((f32[16,32,128]{2,1,0:T(8,128)}), f32[16,32,128]{2,1,0:T(8,128)S(1)}, u32[]{:S(2)}, u32[]{:S(2)}) %all-to-all-start.2) | async-done | bytes 262176 | tf_op jit(solution)/shard_map/all_to_all | solution.py:168
  118.7 0.7 shard_map.87
  (1 shorter events, 0.0 us)
Async XLA Ops:
  0.6 0.7 copy-start
  1.3 0.7 copy-start.2
  2.0 0.7 copy-start.4
  4.0 9.6 %copy-start.1 = (bf16[32,80]{1,0:T(8,128)(2,1)S(1)}, bf16[32,80]{1,0:T(8,128)(2,1)}, u32[]{:S(2)}) copy-start(bf16[32,80]{1,0:T(8,128)(2,1)} %feats_ref.2) | copy-start | bytes 15364
  4.0 9.6 %copy-start.3 = (bf16[16,80]{1,0:T(8,128)(2,1)S(1)}, bf16[16,80]{1,0:T(8,128)(2,1)}, u32[]{:S(2)}) copy-start(bf16[16,80]{1,0:T(8,128)(2,1)} %factor_ref.2) | copy-start | bytes 7684
  4.0 18.8 %all-to-all-start.1 = ((bf16[32,48,128]{2,1,0:T(8,128)(2,1)}), bf16[32,48,128]{2,1,0:T(8,128)(2,1)S(1)}, u32[]{:S(2)}, u32[]{:S(2)}) async-start(bf16[32,48,128]{2,1,0:T(8,128)(2,1)} %shard_map.85), calls=%async_computation.1 | async-start | bytes 786432 | tf_op jit(solution)/shard_map/all_to_all | solution.py:168
  13.6 38.0 %copy-start.5 = (f32[16]{0:T(128)S(1)}, f32[16]{0:T(128)}, u32[]{:S(2)}) copy-start(f32[16]{0:T(128)} %refs_0_.3) | copy-start | bytes 196
  70.7 24.1 %all-to-all-start.3 = ((f32[32,48,128]{2,1,0:T(8,128)}), f32[32,48,128]{2,1,0:T(8,128)S(1)}, u32[]{:S(2)}, u32[]{:S(2)}) async-start(f32[32,48,128]{2,1,0:T(8,128)} %shard_map.88), calls=%async_computation.3 | async-start | bytes 1572864 | tf_op jit(solution)/shard_map/all_to_all | solution.py:168
  94.8 23.9 %all-to-all-start.2 = ((f32[16,32,128]{2,1,0:T(8,128)}), f32[16,32,128]{2,1,0:T(8,128)S(1)}, u32[]{:S(2)}, u32[]{:S(2)}) async-start(f32[16,32,128]{2,1,0:T(8,128)} %shard_map.86), calls=%async_computation.2 | async-start | bytes 524288 | tf_op jit(solution)/shard_map/all_to_all | solution.py:168

commit v3 on v2

v3 whole, which is shorter than its diff:
```python
import jax
import jax.numpy as jnp
from jax import lax
from jax.experimental import pallas as pl
from jax.experimental.pallas import tpu as pltpu
from jax.sharding import Mesh
from jax.sharding import PartitionSpec as P

RING = ("zh", "zl")
PLANE = ("y", "x")
CORE = "core"
BF16 = jnp.bfloat16
F32 = jnp.float32
VMEM = pl.BlockSpec(memory_space=pltpu.VMEM)
HBM = pl.BlockSpec(memory_space=pltpu.HBM)
LANES = 128


def dot(a, b):
    return jnp.dot(a, b, preferred_element_type=F32)


def inverse_column(rank_ref, width):
    rank = rank_ref.shape[0]
    rows = lax.broadcasted_iota(jnp.int32, (rank, width), 0)
    column = jnp.full((rank, width), rank_ref[0], F32)
    for k in range(1, rank):
        column = jnp.where(rows == k, rank_ref[k], column)
    return 1.0 / column


def pack(feats, factor):
    rows, width = feats.shape
    half = width // 2
    halves = jnp.concatenate([factor[:, :half], factor[:, half:]], 0)
    return jnp.concatenate([feats, halves, jnp.zeros((rows, LANES - width - half), F32)], 1)


def unpack(block, rank, width):
    half = width // 2
    halves = block[:, width : width + half]
    return block[:, :width], jnp.concatenate([halves[:rank], halves[rank:]], 1)


def source_copies_kernel(feats_ref, factor_ref, out_ref):
    block = pack(feats_ref[...].astype(F32), factor_ref[...].astype(F32)).astype(BF16)
    for member in range(out_ref.shape[0]):
        out_ref[member] = block


def target_copies_kernel(rank_hbm, feats_hbm, factor_hbm, out_ref, inverse_ref, rank_ref, feats_ref, factor_ref, sems):
    pairs = [(rank_hbm, rank_ref), (feats_hbm, feats_ref), (factor_hbm, factor_ref)]
    loads = [pltpu.make_async_copy(a, b, sems.at[k]) for k, (a, b) in enumerate(pairs)]
    for load in loads:
        load.start()
    for load in loads:
        load.wait()
    factor = factor_ref[...]
    inverse_g = inverse_column(rank_ref, factor.shape[1])
    inverse_ref[...] = inverse_g
    scaled = (factor.astype(F32) * inverse_g).astype(BF16)
    block = jnp.concatenate([feats_ref[...], scaled], 0)
    for member in range(out_ref.shape[0]):
        out_ref[member] = block


def three_parts(value):
    high = value.astype(BF16).astype(F32)
    rest = value - high
    mid = rest.astype(BF16).astype(F32)
    low = (rest - mid).astype(BF16).astype(F32)
    return [high, mid, low]


def squares(feats):
    return jnp.sum(jnp.square(feats), 0, keepdims=True)


def put_sublanes(at, x, q, a_ref, gw_ref, gc_ref):
    width = x.shape[1]
    ones = jnp.ones((1, width), F32)
    stack = jnp.concatenate(
        [-2.0 * x, q] + three_parts(squares(x)) + [ones] * 3 + [jnp.zeros((10, width), F32)], 0
    )
    a_ref[at, :] = stack.T.astype(BF16)
    gw_ref[:, at] = jnp.concatenate([x, ones, jnp.zeros((7, width), F32)], 0).astype(gw_ref.dtype)
    gc_ref[:, at] = q.astype(gc_ref.dtype)


def put_lanes(at, x, q, bd_ref, bp_ref):
    features, width = x.shape
    rank = q.shape[0]
    bd_ref[:, at] = jnp.concatenate(
        [x, jnp.zeros((rank, width), F32), jnp.ones((3, width), F32)]
        + three_parts(squares(x) + 1.0)
        + [jnp.zeros((10, width), F32)],
        0,
    ).astype(BF16)
    bp_ref[:, at] = jnp.concatenate(
        [jnp.zeros((features, width), F32), q, jnp.zeros((16, width), F32)], 0
    ).astype(BF16)


def pair_sums(a_ref, gw, gc, bd, bp, step):
    lanes = bd.shape[1]
    sum_w = jnp.zeros((gw.shape[0], lanes), F32)
    sum_c = jnp.zeros((gc.shape[0], lanes), F32)
    for u in range(0, a_ref.shape[0], step):
        a = a_ref[pl.ds(u, step), :]
        s = dot(a, bd)
        p = dot(a, bp)
        r = lax.rsqrt(s)
        sum_w += dot(gw[:, u : u + step], (p * r).astype(BF16))
        sum_c += dot(gc[:, u : u + step], (s * r).astype(BF16))
    return sum_w, sum_c


def feature_gradient(x, sum_w, scale):
    features = x.shape[0]
    return (x * sum_w[features : features + 1] - sum_w[:features]) * scale


def target_prepare_kernel(features, own_ref, other_ref, a_ref, gw_ref, gc_ref, bd_ref, bp_ref):
    count, _, width = own_ref.shape
    for b in range(2 * count):
        block = (own_ref[b] if b < count else other_ref[b - count]).astype(F32)
        at = pl.ds(b * width, width)
        put_sublanes(at, block[:features], block[features:], a_ref, gw_ref, gc_ref)
        put_lanes(at, block[:features], block[features:], bd_ref, bp_ref)


def source_pair_kernel(scale, width, src_ref, a_ref, gw_ref, gc_ref, out_ref, x_ref, q_ref, bd_ref, bp_ref, sum_ref):
    count, features, _ = src_ref.shape
    rank = gc_ref.shape[0]
    for b in range(count):
        x, q = unpack(src_ref[b].astype(F32), rank, width)
        x_ref[:, b * width : (b + 1) * width] = x
        q_ref[:, b * width : (b + 1) * width] = q
    lanes = x_ref.shape[1]
    put_lanes(slice(None), x_ref[...], q_ref[...], bd_ref, bp_ref)
    gw = gw_ref[...]
    gc = gc_ref[...]
    step = lanes // 2
    for start in range(0, lanes, step):
        at = slice(start, start + step)
        sum_w, sum_c = pair_sums(a_ref, gw, gc, bd_ref[:, at], bp_ref[:, at], 1024)
        sum_ref[:features, at] = feature_gradient(x_ref[:, at], sum_w, scale)
        sum_ref[features:, at] = sum_c * scale
    for b in range(count):
        block = sum_ref[:, b * width : (b + 1) * width]
        out_ref[b] = pack(block[:features], block[features:])


def target_pair_kernel(scale, src_width, inverse_ref, src_ref, own_ref, other_ref, bd_ref, bp_ref, keep_ref, send_ref, a_ref, gw_ref, gc_ref):
    src_count, features, _ = src_ref.shape
    rank = own_ref.shape[1] - features
    for b in range(src_count):
        x, q = unpack(src_ref[b].astype(F32), rank, src_width)
        put_sublanes(pl.ds(b * src_width, src_width), x, q, a_ref, gw_ref, gc_ref)
    gw = gw_ref[...].astype(BF16)
    gc = gc_ref[...].astype(BF16)
    count, _, width = own_ref.shape
    factor_scale = inverse_ref[...] * scale
    group = 8
    step = group * width
    for half, (from_ref, to_ref) in enumerate([(own_ref, keep_ref), (other_ref, send_ref)]):

        def advance(index, carry):
            at = pl.ds(pl.multiple_of(half * count * width + index * step, step), step)
            sum_w, sum_c = pair_sums(a_ref, gw, gc, bd_ref[:, at], bp_ref[:, at], a_ref.shape[0] // 2)
            for k in range(group):
                lanes = slice(k * width, (k + 1) * width)
                x = from_ref[index * group + k][:features].astype(F32)
                grad = feature_gradient(x, sum_w[:, lanes], scale)
                to_ref[index * group + k] = jnp.concatenate([grad, sum_c[:, lanes] * factor_scale], 0)
            return carry

        lax.fori_loop(0, count // group, advance, 0)


def target_sum_kernel(features, parts_ref, feats_ref, factor_ref):
    total = jnp.sum(parts_ref[...], 0)
    feats_ref[...] = total[:features]
    factor_ref[...] = total[features:]


def source_sum_kernel(parts_ref, feats_ref, factor_ref):
    rank, width = factor_ref.shape
    feats, factor = unpack(jnp.sum(parts_ref[...], 0), rank, width)
    feats_ref[...] = feats
    factor_ref[...] = factor


def call(kernel, specs, outs, scratch=(), flops=0):
    single = not isinstance(outs, tuple)
    return pl.pallas_call(
        kernel,
        out_shape=outs,
        in_specs=specs,
        out_specs=VMEM if single else tuple(VMEM for _ in outs),
        scratch_shapes=scratch,
        compiler_params=pltpu.CompilerParams(vmem_limit_bytes=40 << 20),
        cost_estimate=pl.CostEstimate(flops=flops, transcendentals=0, bytes_accessed=1 << 20),
    )


def shape(*dims, dtype=F32):
    return jax.ShapeDtypeStruct(dims, dtype)


def exchange(blocks, axes):
    return lax.all_to_all(blocks, axes, 0, 0, tiled=True)


def swap(blocks):
    return lax.ppermute(blocks, CORE, [(0, 1), (1, 0)])


def local(src_feats, src_factor, tgt_feats, tgt_factor, rank_weight):
    features, src_width = src_feats.shape
    rank = src_factor.shape[0]
    rows = features + rank
    tgt_width = tgt_feats.shape[1]
    ring = lax.axis_size(RING)
    plane = lax.axis_size(PLANE)
    scale = 1.0 / (tgt_width * ring * plane * lax.axis_size(CORE))
    sources = ring * src_width
    targets = 2 * plane * tgt_width

    tgt_copies, inverse_g = call(
        target_copies_kernel,
        (HBM,) * 3,
        (shape(plane, rows, tgt_width, dtype=BF16), shape(rank, tgt_width)),
        (
            pltpu.SMEM((rank,), F32),
            pltpu.VMEM((features, tgt_width), BF16),
            pltpu.VMEM((rank, tgt_width), BF16),
            pltpu.SemaphoreType.DMA((3,)),
        ),
    )(*(pltpu.with_memory_space_constraint(array, pltpu.HBM) for array in (rank_weight, tgt_feats, tgt_factor)))
    src_copies = call(source_copies_kernel, (VMEM, VMEM), shape(ring, features, LANES, dtype=BF16))(
        src_feats, src_factor
    )
    tgt_own = exchange(tgt_copies, PLANE)
    tgt_own, src_copies = lax.optimization_barrier((tgt_own, src_copies))
    src_blocks = exchange(src_copies, RING)
    tgt_other = swap(tgt_own)

    a, gw, gc, bd, bp = call(
        lambda *refs: target_prepare_kernel(features, *refs),
        (VMEM, VMEM),
        (
            shape(targets, 64, dtype=BF16),
            shape(features + 8, targets, dtype=BF16),
            shape(rank, targets, dtype=BF16),
            shape(64, targets, dtype=BF16),
            shape(64, targets, dtype=BF16),
        ),
        flops=1 << 22,
    )(tgt_own, tgt_other)

    flops = sources * targets * 2 * 256 * 4
    src_parts = call(
        lambda *refs: source_pair_kernel(scale, src_width, *refs),
        (VMEM,) * 4,
        shape(ring, features, LANES),
        (
            pltpu.VMEM((features, sources), F32),
            pltpu.VMEM((rank, sources), F32),
            pltpu.VMEM((64, sources), BF16),
            pltpu.VMEM((64, sources), BF16),
            pltpu.VMEM((rows, sources), F32),
        ),
        flops,
    )(src_blocks, a, gw, gc)
    src_sums = exchange(src_parts, RING)
    keep, send = call(
        lambda *refs: target_pair_kernel(scale, src_width, *refs),
        (VMEM,) * 6,
        (shape(plane, rows, tgt_width), shape(plane, rows, tgt_width)),
        (
            pltpu.VMEM((sources, 64), BF16),
            pltpu.VMEM((features + 8, sources), F32),
            pltpu.VMEM((rank, sources), F32),
        ),
        flops,
    )(inverse_g, src_blocks, tgt_own, tgt_other, bd, bp)
    src_sums, tgt_half = lax.optimization_barrier((src_sums, keep + swap(send)))
    tgt_sums = exchange(tgt_half, PLANE)

    grad_x, grad_q = call(source_sum_kernel, (VMEM,), (shape(features, src_width), shape(rank, src_width)))(src_sums)
    grad_y, grad_r = call(
        lambda *refs: target_sum_kernel(features, *refs), (VMEM,), (shape(features, tgt_width), shape(rank, tgt_width))
    )(tgt_sums)
    return grad_x, grad_q, grad_y, grad_r


def solution(mesh):
    fine = Mesh(mesh.devices.reshape(8, 2, 2, 4, 4), ("zl", "core", "zh", "y", "x"))
    by_src = P(None, ("zl", "core", "zh", "y", "x"))
    by_tgt = P(None, ("zh", "y", "x", "zl", "core"))
    return jax.shard_map(
        local,
        mesh=fine,
        in_specs=(by_src, by_src, by_tgt, by_tgt, P()),
        out_specs=(by_src, by_src, by_tgt, by_tgt),
        check_vma=False,
    )
```

time: 120 us -> 91.1 us (0.76)
  the two profiles are of different devices: /device:TPU:2 before, /device:TPU:32 now
where the time goes in v3:
time: 91.1 us; the launch traced here: 90.6 us
  starting transfers between devices  34.3 us (38%)
  waiting for transfers between devices  31.2 us (34%)
  Pallas kernels  23.6 us (26%)
    all_to_all x4, starting transfers between devices, exchange(): return lax.all_to_all(blocks, axes, 0, 0, tiled=True)  30.5 us
    all_to_all x4, waiting for transfers between devices, exchange(): return lax.all_to_all(blocks, axes, 0, 0, tiled=True)  28.1 us
    pallas_call x1, Pallas kernels, local(): call(lambda *refs: target_pair_kernel(scale, src_width, *refs), (VMEM,) *...  10.1 us
    pallas_call x1, Pallas kernels, local(): call(lambda *refs: source_pair_kernel(scale, src_width, *refs), (VMEM,) *...  9.38 us
    ppermute x2, starting transfers between devices, swap(): return lax.ppermute(blocks, CORE, [(0, 1), (1, 0)])  3.83 us
    ppermute x2, waiting for transfers between devices, swap(): return lax.ppermute(blocks, CORE, [(0, 1), (1, 0)])  3.1 us
  transfers between devices with their start and end apart: 6, of which 6 were waited for; matrix products, arithmetic and copies ran while one was open for 1% of the time, Pallas kernels for 13%

profile of v3, /device:TPU:32, one launch (start us, length us, event | category | flops | bytes accessed | tf_op | source)
XLA Modules:
  0.0 90.6 jit_solution(13461335634201018235)
XLA Ops:
  0.6 1.4 %shard_map.84 = (bf16[16,48,128]{2,1,0:T(8,128)(2,1)}, f32[16,128]{1,0:T(8,128)S(1)}) custom-call(f32[16]{0:T(128)} %rank_hbm.1, bf16[32,128]{1,0:T(8,128)(2,1)} %feats_hbm.1, bf16[16,128]{1,0:T(8,128)(2,1)} %factor_hbm.1), custom_call_target="tpu_custom_call" | custom-call | bytes 1048576 | tf_op jit(solution)/shard_map/pallas_call | solution.py:230
  2.1 0.0 copy-start
  2.1 0.0 copy-start.1
  2.1 7.0 %all-to-all-start = ((bf16[16,48,128]{2,1,0:T(8,128)(2,1)}), bf16[16,48,128]{2,1,0:T(8,128)(2,1)S(1)}, u32[]{:S(2)}, u32[]{:S(2)}) async-start(bf16[16,48,128]{2,1,0:T(8,128)(2,1)} %get-tuple-element.21), calls=%async_computation | async-start | bytes 393216 | tf_op jit(solution)/shard_map/all_to_all | solution.py:212
  9.1 0.0 copy-done
  9.2 0.0 copy-done.1
  9.2 0.8 shard_map.85
  10.0 7.5 %all-to-all-done.refs_0_.refs_2_ = bf16[16,48,128]{2,1,0:T(8,128)(2,1)S(1)} async-done(((bf16[16,48,128]{2,1,0:T(8,128)(2,1)}), bf16[16,48,128]{2,1,0:T(8,128)(2,1)S(1)}, u32[]{:S(2)}, u32[]{:S(2)}) %all-to-all-start) | async-done | bytes 196640 | tf_op jit(solution)/shard_map/all_to_all | solution.py:212
  17.5 15.2 %all-to-all-start.1 = ((bf16[16,32,128]{2,1,0:T(8,128)(2,1)}), bf16[16,32,128]{2,1,0:T(8,128)(2,1)S(1)}, u32[]{:S(2)}, u32[]{:S(2)}) async-start(bf16[16,32,128]{2,1,0:T(8,128)(2,1)} %shard_map.85), calls=%async_computation.1 | async-start | bytes 262144 | tf_op jit(solution)/shard_map/all_to_all | solution.py:212
  32.7 1.9 %collective-permute-start = (bf16[16,48,128]{2,1,0:T(8,128)(2,1)S(1)}, bf16[16,48,128]{2,1,0:T(8,128)(2,1)S(1)}, u32[]{:S(2)}, u32[]{:S(2)}) collective-permute-start(bf16[16,48,128]{2,1,0:T(8,128)(2,1)S(1)} %all-to-all-done.refs_0_.refs_2_), channel_id=1, source_target_pairs={{0,32},{32,0},{1,33},{33,1},{2,34},{34,2},{3,35},{35,3},{4,36},{36... | collective-permute-start | bytes 589832 | tf_op jit(solution)/shard_map/ppermute | solution.py:216
  34.6 1.4 %collective-permute-done.refs_1_.refs_3_ = bf16[16,48,128]{2,1,0:T(8,128)(2,1)S(1)} collective-permute-done((bf16[16,48,128]{2,1,0:T(8,128)(2,1)S(1)}, bf16[16,48,128]{2,1,0:T(8,128)(2,1)S(1)}, u32[]{:S(2)}, u32[]{:S(2)}) %collective-permute-start) | collective-permute-done | bytes 196640 | tf_op jit(solution)/shard_map/ppermute | solution.py:216
  36.0 0.5 shard_map.86
  36.5 8.7 %all-to-all-done.1.refs_0_.refs_1_ = bf16[16,32,128]{2,1,0:T(8,128)(2,1)S(1)} async-done(((bf16[16,32,128]{2,1,0:T(8,128)(2,1)}), bf16[16,32,128]{2,1,0:T(8,128)(2,1)S(1)}, u32[]{:S(2)}, u32[]{:S(2)}) %all-to-all-start.1) | async-done | bytes 131104 | tf_op jit(solution)/shard_map/all_to_all | solution.py:212
  45.2 9.4 %shard_map.87 = f32[16,32,128]{2,1,0:T(8,128)} custom-call(bf16[16,32,128]{2,1,0:T(8,128)(2,1)S(1)} %all-to-all-done.1.refs_0_.refs_1_, bf16[4096,64]{1,0:T(8,128)(2,1)S(1)} %get-tuple-element.24.refs_1_, bf16[40,4096]{1,0:T(8,128)(2,1)S(1)} %get-tuple-element.25.refs_2_, bf16[16,4096]{1,0:T(8,128)(2,1)S(1)} %get-tuple-element.26.refs_3_), custom_call_target="tpu_custom_call" | custom-call | flops 10737418240 | bytes 1048576 | tf_op jit(solution)/shard_map/pallas_call | solution.py:263
  54.6 4.6 %all-to-all-start.2 = ((f32[16,32,128]{2,1,0:T(8,128)}), f32[16,32,128]{2,1,0:T(8,128)S(1)}, u32[]{:S(2)}, u32[]{:S(2)}) async-start(f32[16,32,128]{2,1,0:T(8,128)} %shard_map.87), calls=%async_computation.2 | async-start | bytes 524288 | tf_op jit(solution)/shard_map/all_to_all | solution.py:212
  59.2 10.1 %shard_map.88 = (f32[16,48,128]{2,1,0:T(8,128)S(1)}, f32[16,48,128]{2,1,0:T(8,128)S(1)}) custom-call(f32[16,128]{1,0:T(8,128)S(1)} %get-tuple-element.27.refs_0_, bf16[16,32,128]{2,1,0:T(8,128)(2,1)S(1)} %all-to-all-done.1.refs_0_.refs_1_, bf16[16,48,128]{2,1,0:T(8,128)(2,1)S(1)} %all-to-all-done.refs_0_.refs_2_, ...), custom_call_target="tpu_custom_call" | custom-call | flops 10737418240 | bytes 1048576 | tf_op jit(solution)/shard_map/pallas_call | solution.py:277
  69.4 1.9 %collective-permute-start.1 = (f32[16,48,128]{2,1,0:T(8,128)S(1)}, f32[16,48,128]{2,1,0:T(8,128)S(1)}, u32[]{:S(2)}, u32[]{:S(2)}) collective-permute-start(f32[16,48,128]{2,1,0:T(8,128)S(1)} %get-tuple-element.31), channel_id=1, source_target_pairs={{0,32},{32,0},{1,33},{33,1},{2,34},{34,2},{3,35},{35,3},{4,36},{36... | collective-permute-start | bytes 1179656 | tf_op jit(solution)/shard_map/ppermute | solution.py:216
  71.3 1.7 %collective-permute-done.1 = f32[16,48,128]{2,1,0:T(8,128)S(1)} collective-permute-done((f32[16,48,128]{2,1,0:T(8,128)S(1)}, f32[16,48,128]{2,1,0:T(8,128)S(1)}, u32[]{:S(2)}, u32[]{:S(2)}) %collective-permute-start.1) | collective-permute-done | bytes 393248 | tf_op jit(solution)/shard_map/ppermute | solution.py:216
  73.0 0.8 add.3
  73.8 3.2 %all-to-all-done.2.parts_ref = f32[16,32,128]{2,1,0:T(8,128)S(1)} async-done(((f32[16,32,128]{2,1,0:T(8,128)}), f32[16,32,128]{2,1,0:T(8,128)S(1)}, u32[]{:S(2)}, u32[]{:S(2)}) %all-to-all-start.2) | async-done | bytes 262176 | tf_op jit(solution)/shard_map/all_to_all | solution.py:212
  77.0 3.6 %all-to-all-start.3 = ((f32[16,48,128]{2,1,0:T(8,128)}), f32[16,48,128]{2,1,0:T(8,128)S(1)}, u32[]{:S(2)}, u32[]{:S(2)}) async-start(f32[16,48,128]{2,1,0:T(8,128)} %add.3), calls=%async_computation.3 | async-start | bytes 786432 | tf_op jit(solution)/shard_map/all_to_all | solution.py:212
  80.6 0.7 shard_map.89
  81.3 8.7 %all-to-all-done.3.refs_0_ = f32[16,48,128]{2,1,0:T(8,128)S(1)} async-done(((f32[16,48,128]{2,1,0:T(8,128)}), f32[16,48,128]{2,1,0:T(8,128)S(1)}, u32[]{:S(2)}, u32[]{:S(2)}) %all-to-all-start.3) | async-done | bytes 393248 | tf_op jit(solution)/shard_map/all_to_all | solution.py:212
  89.9 0.6 shard_map.90
Async XLA Ops:
  2.1 7.1 %copy-start = (bf16[32,80]{1,0:T(8,128)(2,1)S(1)}, bf16[32,80]{1,0:T(8,128)(2,1)}, u32[]{:S(2)}) copy-start(bf16[32,80]{1,0:T(8,128)(2,1)} %feats_ref.1) | copy-start | bytes 15364
  2.1 7.1 %copy-start.1 = (bf16[16,80]{1,0:T(8,128)(2,1)S(1)}, bf16[16,80]{1,0:T(8,128)(2,1)}, u32[]{:S(2)}) copy-start(bf16[16,80]{1,0:T(8,128)(2,1)} %factor_ref.1) | copy-start | bytes 7684
  2.1 15.4 %all-to-all-start = ((bf16[16,48,128]{2,1,0:T(8,128)(2,1)}), bf16[16,48,128]{2,1,0:T(8,128)(2,1)S(1)}, u32[]{:S(2)}, u32[]{:S(2)}) async-start(bf16[16,48,128]{2,1,0:T(8,128)(2,1)} %get-tuple-element.21), calls=%async_computation | async-start | bytes 393216 | tf_op jit(solution)/shard_map/all_to_all | solution.py:212
  17.5 27.7 %all-to-all-start.1 = ((bf16[16,32,128]{2,1,0:T(8,128)(2,1)}), bf16[16,32,128]{2,1,0:T(8,128)(2,1)S(1)}, u32[]{:S(2)}, u32[]{:S(2)}) async-start(bf16[16,32,128]{2,1,0:T(8,128)(2,1)} %shard_map.85), calls=%async_computation.1 | async-start | bytes 262144 | tf_op jit(solution)/shard_map/all_to_all | solution.py:212
  32.7 3.3 %collective-permute-start = (bf16[16,48,128]{2,1,0:T(8,128)(2,1)S(1)}, bf16[16,48,128]{2,1,0:T(8,128)(2,1)S(1)}, u32[]{:S(2)}, u32[]{:S(2)}) collective-permute-start(bf16[16,48,128]{2,1,0:T(8,128)(2,1)S(1)} %all-to-all-done.refs_0_.refs_2_), channel_id=1, source_target_pairs={{0,32},{32,0},{1,33},{33,1},{2,34},{34,2},{3,35},{35,3},{4,36},{36... | collective-permute-start | bytes 589832 | tf_op jit(solution)/shard_map/ppermute | solution.py:216
  54.6 22.4 %all-to-all-start.2 = ((f32[16,32,128]{2,1,0:T(8,128)}), f32[16,32,128]{2,1,0:T(8,128)S(1)}, u32[]{:S(2)}, u32[]{:S(2)}) async-start(f32[16,32,128]{2,1,0:T(8,128)} %shard_map.87), calls=%async_computation.2 | async-start | bytes 524288 | tf_op jit(solution)/shard_map/all_to_all | solution.py:212
  69.4 3.6 %collective-permute-start.1 = (f32[16,48,128]{2,1,0:T(8,128)S(1)}, f32[16,48,128]{2,1,0:T(8,128)S(1)}, u32[]{:S(2)}, u32[]{:S(2)}) collective-permute-start(f32[16,48,128]{2,1,0:T(8,128)S(1)} %get-tuple-element.31), channel_id=1, source_target_pairs={{0,32},{32,0},{1,33},{33,1},{2,34},{34,2},{3,35},{35,3},{4,36},{36... | collective-permute-start | bytes 1179656 | tf_op jit(solution)/shard_map/ppermute | solution.py:216
  77.0 12.9 %all-to-all-start.3 = ((f32[16,48,128]{2,1,0:T(8,128)}), f32[16,48,128]{2,1,0:T(8,128)S(1)}, u32[]{:S(2)}, u32[]{:S(2)}) async-start(f32[16,48,128]{2,1,0:T(8,128)} %add.3), calls=%async_computation.3 | async-start | bytes 786432 | tf_op jit(solution)/shard_map/all_to_all | solution.py:212

commit v4 on v3

--- a/solution.py
+++ b/solution.py
@@ -120,13 +120,15 @@
     return (x * sum_w[features : features + 1] - sum_w[:features]) * scale
 
 
-def target_prepare_kernel(features, own_ref, other_ref, a_ref, gw_ref, gc_ref, bd_ref, bp_ref):
+def target_prepare_kernel(features, own_ref, other_ref, a_ref, gw_ref, gc_ref, own_bd, own_bp, other_bd, other_bp):
     count, _, width = own_ref.shape
-    for b in range(2 * count):
-        block = (own_ref[b] if b < count else other_ref[b - count]).astype(F32)
-        at = pl.ds(b * width, width)
-        put_sublanes(at, block[:features], block[features:], a_ref, gw_ref, gc_ref)
-        put_lanes(at, block[:features], block[features:], bd_ref, bp_ref)
+    for half, (ref, bd_ref, bp_ref) in enumerate([(own_ref, own_bd, own_bp), (other_ref, other_bd, other_bp)]):
+        for b in range(count):
+            block = ref[b].astype(F32)
+            put_sublanes(
+                pl.ds((half * count + b) * width, width), block[:features], block[features:], a_ref, gw_ref, gc_ref
+            )
+            put_lanes(pl.ds(b * width, width), block[:features], block[features:], bd_ref, bp_ref)
 
 
 def source_pair_kernel(scale, width, src_ref, a_ref, gw_ref, gc_ref, out_ref, x_ref, q_ref, bd_ref, bp_ref, sum_ref):
@@ -148,45 +150,53 @@
         sum_ref[features:, at] = sum_c * scale
     for b in range(count):
         block = sum_ref[:, b * width : (b + 1) * width]
-        out_ref[b] = pack(block[:features], block[features:])
-
-
-def target_pair_kernel(scale, src_width, inverse_ref, src_ref, own_ref, other_ref, bd_ref, bp_ref, keep_ref, send_ref, a_ref, gw_ref, gc_ref):
-    src_count, features, _ = src_ref.shape
-    rank = own_ref.shape[1] - features
-    for b in range(src_count):
-        x, q = unpack(src_ref[b].astype(F32), rank, src_width)
-        put_sublanes(pl.ds(b * src_width, src_width), x, q, a_ref, gw_ref, gc_ref)
-    gw = gw_ref[...].astype(BF16)
-    gc = gc_ref[...].astype(BF16)
-    count, _, width = own_ref.shape
+        out_ref[b] = pack(block[:features], block[features:]).astype(out_ref.dtype)
+
+
+def target_chunks(scale, inverse_ref, from_ref, a_ref, gw, gc, bd_ref, bp_ref, to_ref):
+    count, rows, width = from_ref.shape
+    features = rows - gc.shape[0]
     factor_scale = inverse_ref[...] * scale
     group = 8
     step = group * width
-    for half, (from_ref, to_ref) in enumerate([(own_ref, keep_ref), (other_ref, send_ref)]):
-
-        def advance(index, carry):
-            at = pl.ds(pl.multiple_of(half * count * width + index * step, step), step)
-            sum_w, sum_c = pair_sums(a_ref, gw, gc, bd_ref[:, at], bp_ref[:, at], a_ref.shape[0] // 2)
-            for k in range(group):
-                lanes = slice(k * width, (k + 1) * width)
-                x = from_ref[index * group + k][:features].astype(F32)
-                grad = feature_gradient(x, sum_w[:, lanes], scale)
-                to_ref[index * group + k] = jnp.concatenate([grad, sum_c[:, lanes] * factor_scale], 0)
-            return carry
-
-        lax.fori_loop(0, count // group, advance, 0)
+
+    def advance(index, carry):
+        at = pl.ds(pl.multiple_of(index * step, step), step)
+        sum_w, sum_c = pair_sums(a_ref, gw, gc, bd_ref[:, at], bp_ref[:, at], a_ref.shape[0] // 2)
+        for k in range(group):
+            lanes = slice(k * width, (k + 1) * width)
+            x = from_ref[index * group + k][:features].astype(F32)
+            grad = feature_gradient(x, sum_w[:, lanes], scale)
+            to_ref[index * group + k] = jnp.concatenate([grad, sum_c[:, lanes] * factor_scale], 0)
+        return carry
+
+    lax.fori_loop(0, count // group, advance, 0)
+
+
+def first_target_kernel(scale, src_width, inverse_ref, src_ref, tgt_ref, bd_ref, bp_ref, out_ref, a_ref, gw_ref, gc_ref, gw32_ref, gc32_ref):
+    src_count = src_ref.shape[0]
+    rank = gc_ref.shape[0]
+    for b in range(src_count):
+        x, q = unpack(src_ref[b].astype(F32), rank, src_width)
+        put_sublanes(pl.ds(b * src_width, src_width), x, q, a_ref, gw32_ref, gc32_ref)
+    gw_ref[...] = gw32_ref[...].astype(BF16)
+    gc_ref[...] = gc32_ref[...].astype(BF16)
+    target_chunks(scale, inverse_ref, tgt_ref, a_ref, gw_ref[...], gc_ref[...], bd_ref, bp_ref, out_ref)
+
+
+def second_target_kernel(scale, inverse_ref, tgt_ref, bd_ref, bp_ref, a_ref, gw_ref, gc_ref, out_ref):
+    target_chunks(scale, inverse_ref, tgt_ref, a_ref, gw_ref[...], gc_ref[...], bd_ref, bp_ref, out_ref)
 
 
 def target_sum_kernel(features, parts_ref, feats_ref, factor_ref):
-    total = jnp.sum(parts_ref[...], 0)
+    total = jnp.sum(parts_ref[...].astype(F32), 0)
     feats_ref[...] = total[:features]
     factor_ref[...] = total[features:]
 
 
 def source_sum_kernel(parts_ref, feats_ref, factor_ref):
     rank, width = factor_ref.shape
-    feats, factor = unpack(jnp.sum(parts_ref[...], 0), rank, width)
+    feats, factor = unpack(jnp.sum(parts_ref[...].astype(F32), 0), rank, width)
     feats_ref[...] = feats
     factor_ref[...] = factor
 
@@ -246,16 +256,16 @@
     src_blocks = exchange(src_copies, RING)
     tgt_other = swap(tgt_own)
 
-    a, gw, gc, bd, bp = call(
+    half = plane * tgt_width
+    a, gw, gc, own_bd, own_bp, other_bd, other_bp = call(
         lambda *refs: target_prepare_kernel(features, *refs),
         (VMEM, VMEM),
         (
             shape(targets, 64, dtype=BF16),
             shape(features + 8, targets, dtype=BF16),
             shape(rank, targets, dtype=BF16),
-            shape(64, targets, dtype=BF16),
-            shape(64, targets, dtype=BF16),
-        ),
+        )
+        + (shape(64, half, dtype=BF16),) * 4,
         flops=1 << 22,
     )(tgt_own, tgt_other)
 
@@ -263,7 +273,7 @@
     src_parts = call(
         lambda *refs: source_pair_kernel(scale, src_width, *refs),
         (VMEM,) * 4,
-        shape(ring, features, LANES),
+        shape(ring, features, LANES, dtype=BF16),
         (
             pltpu.VMEM((features, sources), F32),
             pltpu.VMEM((rank, sources), F32),
@@ -274,18 +284,26 @@
         flops,
     )(src_blocks, a, gw, gc)
     src_sums = exchange(src_parts, RING)
-    keep, send = call(
-        lambda *refs: target_pair_kernel(scale, src_width, *refs),
-        (VMEM,) * 6,
-        (shape(plane, rows, tgt_width), shape(plane, rows, tgt_width)),
+    send, src_a, src_gw, src_gc = call(
+        lambda *refs: first_target_kernel(scale, src_width, *refs),
+        (VMEM,) * 5,
         (
-            pltpu.VMEM((sources, 64), BF16),
-            pltpu.VMEM((features + 8, sources), F32),
-            pltpu.VMEM((rank, sources), F32),
+            shape(plane, rows, tgt_width),
+            shape(sources, 64, dtype=BF16),
+            shape(features + 8, sources, dtype=BF16),
+            shape(rank, sources, dtype=BF16),
         ),
-        flops,
-    )(inverse_g, src_blocks, tgt_own, tgt_other, bd, bp)
-    src_sums, tgt_half = lax.optimization_barrier((src_sums, keep + swap(send)))
+        (pltpu.VMEM((features + 8, sources), F32), pltpu.VMEM((rank, sources), F32)),
+        flops // 2,
+    )(inverse_g, src_blocks, tgt_other, other_bd, other_bp)
+    received = swap(send)
+    keep = call(
+        lambda *refs: second_target_kernel(scale, *refs),
+        (VMEM,) * 7,
+        shape(plane, rows, tgt_width),
+        flops=flops // 2,
+    )(inverse_g, tgt_own, own_bd, own_bp, src_a, src_gw, src_gc)
+    src_sums, tgt_half = lax.optimization_barrier((src_sums, (keep + received).astype(BF16)))
     tgt_sums = exchange(tgt_half, PLANE)
 
     grad_x, grad_q = call(source_sum_kernel, (VMEM,), (shape(features, src_width), shape(rank, src_width)))(src_sums)

time: 91.1 us -> 85.7 us (0.941)
  waiting for transfers between devices: 31.2 us -> 25.8 us
    all_to_all x4, waiting for transfers between devices: 28.1 us -> 24.4 us  [exchange(): return lax.all_to_all(blocks, axes, 0, 0, tiled=True)]
    ppermute x2, waiting for transfers between devices: 3.1 us -> 1.41 us  [swap(): return lax.ppermute(blocks, CORE, [(0, 1), (1, 0)])]
    pallas_call x1 -> x2, Pallas kernels: 10.1 us -> 10.2 us  [the longest x1 5.6 us: local(): call(lambda *refs: first_target_kernel(scale, src_width, *refs), (VMEM,)...]
  transfers between devices with their start and end apart: 6 -> 6, of which waited for: 6 -> 4; matrix products, arithmetic and copies ran while one was open for 1% -> 1% of each run, Pallas kernels for 13% -> 14%
where the time goes in v4:
time: 85.7 us; the launch traced here: 85.1 us
  starting transfers between devices  34.3 us (40%)
  waiting for transfers between devices  25.8 us (30%)
  Pallas kernels  23.6 us (28%)
    all_to_all x4, starting transfers between devices, exchange(): return lax.all_to_all(blocks, axes, 0, 0, tiled=True)  30.4 us
    all_to_all x4, waiting for transfers between devices, exchange(): return lax.all_to_all(blocks, axes, 0, 0, tiled=True)  24.4 us
    pallas_call x1, Pallas kernels, local(): call(lambda *refs: source_pair_kernel(scale, src_width, *refs), (VMEM,) *...  9.35 us
    pallas_call x1, Pallas kernels, local(): call(lambda *refs: first_target_kernel(scale, src_width, *refs), (VMEM,)...  5.6 us
    pallas_call x1, Pallas kernels, local(): call(lambda *refs: second_target_kernel(scale, *refs), (VMEM,) * 7, shape...  4.56 us
    ppermute x2, starting transfers between devices, swap(): return lax.ppermute(blocks, CORE, [(0, 1), (1, 0)])  3.83 us
  transfers between devices with their start and end apart: 6, of which 4 were waited for; matrix products, arithmetic and copies ran while one was open for 1% of the time, Pallas kernels for 14%

profile of v4, /device:TPU:32, one launch (start us, length us, event | category | flops | bytes accessed | tf_op | source)
XLA Modules:
  0.0 85.1 jit_solution(12873436338494260934)
XLA Ops:
  0.6 1.4 %shard_map.84 = (bf16[16,48,128]{2,1,0:T(8,128)(2,1)}, f32[16,128]{1,0:T(8,128)S(1)}) custom-call(f32[16]{0:T(128)} %rank_hbm.1, bf16[32,128]{1,0:T(8,128)(2,1)} %feats_hbm.1, bf16[16,128]{1,0:T(8,128)(2,1)} %factor_hbm.1), custom_call_target="tpu_custom_call" | custom-call | bytes 1048576 | tf_op jit(solution)/shard_map/pallas_call | solution.py:240
  2.1 0.0 copy-start
  2.1 0.0 copy-start.1
  2.1 7.0 %all-to-all-start = ((bf16[16,48,128]{2,1,0:T(8,128)(2,1)}), bf16[16,48,128]{2,1,0:T(8,128)(2,1)S(1)}, u32[]{:S(2)}, u32[]{:S(2)}) async-start(bf16[16,48,128]{2,1,0:T(8,128)(2,1)} %get-tuple-element.25), calls=%async_computation | async-start | bytes 393216 | tf_op jit(solution)/shard_map/all_to_all | solution.py:222
  9.1 0.0 copy-done
  9.2 0.0 copy-done.1
  9.2 0.8 shard_map.85
  10.0 7.5 %all-to-all-done.refs_0_.refs_1_ = bf16[16,48,128]{2,1,0:T(8,128)(2,1)S(1)} async-done(((bf16[16,48,128]{2,1,0:T(8,128)(2,1)}), bf16[16,48,128]{2,1,0:T(8,128)(2,1)S(1)}, u32[]{:S(2)}, u32[]{:S(2)}) %all-to-all-start) | async-done | bytes 196640 | tf_op jit(solution)/shard_map/all_to_all | solution.py:222
  17.5 15.2 %all-to-all-start.1 = ((bf16[16,32,128]{2,1,0:T(8,128)(2,1)}), bf16[16,32,128]{2,1,0:T(8,128)(2,1)S(1)}, u32[]{:S(2)}, u32[]{:S(2)}) async-start(bf16[16,32,128]{2,1,0:T(8,128)(2,1)} %shard_map.85), calls=%async_computation.1 | async-start | bytes 262144 | tf_op jit(solution)/shard_map/all_to_all | solution.py:222
  32.7 1.9 %collective-permute-start = (bf16[16,48,128]{2,1,0:T(8,128)(2,1)S(1)}, bf16[16,48,128]{2,1,0:T(8,128)(2,1)S(1)}, u32[]{:S(2)}, u32[]{:S(2)}) collective-permute-start(bf16[16,48,128]{2,1,0:T(8,128)(2,1)S(1)} %all-to-all-done.refs_0_.refs_1_), channel_id=1, source_target_pairs={{0,32},{32,0},{1,33},{33,1},{2,34},{34,2},{3,35},{35,3},{4,36},{36... | collective-permute-start | bytes 589832 | tf_op jit(solution)/shard_map/ppermute | solution.py:226
  34.6 1.4 %collective-permute-done.refs_1_.refs_2_ = bf16[16,48,128]{2,1,0:T(8,128)(2,1)S(1)} collective-permute-done((bf16[16,48,128]{2,1,0:T(8,128)(2,1)S(1)}, bf16[16,48,128]{2,1,0:T(8,128)(2,1)S(1)}, u32[]{:S(2)}, u32[]{:S(2)}) %collective-permute-start) | collective-permute-done | bytes 196640 | tf_op jit(solution)/shard_map/ppermute | solution.py:226
  36.0 0.5 shard_map.86
  36.5 8.7 %all-to-all-done.1.refs_0_.refs_1_ = bf16[16,32,128]{2,1,0:T(8,128)(2,1)S(1)} async-done(((bf16[16,32,128]{2,1,0:T(8,128)(2,1)}), bf16[16,32,128]{2,1,0:T(8,128)(2,1)S(1)}, u32[]{:S(2)}, u32[]{:S(2)}) %all-to-all-start.1) | async-done | bytes 131104 | tf_op jit(solution)/shard_map/all_to_all | solution.py:222
  45.2 9.4 %shard_map.87 = bf16[16,32,128]{2,1,0:T(8,128)(2,1)} custom-call(bf16[16,32,128]{2,1,0:T(8,128)(2,1)S(1)} %all-to-all-done.1.refs_0_.refs_1_, bf16[4096,64]{1,0:T(8,128)(2,1)S(1)} %get-tuple-element.28.refs_1_, bf16[40,4096]{1,0:T(8,128)(2,1)S(1)} %get-tuple-element.29.refs_2_, bf16[16,4096]{1,0:T(8,128)(2,1)S(1)} %get-tuple-element.30.refs_3_), custom_call_target="tpu_custom_call" | custom-call | flops 10737418240 | bytes 1048576 | tf_op jit(solution)/shard_map/pallas_call | solution.py:273
  54.6 4.6 %all-to-all-start.2 = ((bf16[16,32,128]{2,1,0:T(8,128)(2,1)}), bf16[16,32,128]{2,1,0:T(8,128)(2,1)S(1)}, u32[]{:S(2)}, u32[]{:S(2)}) async-start(bf16[16,32,128]{2,1,0:T(8,128)(2,1)} %shard_map.87), calls=%async_computation.2 | async-start | bytes 262144 | tf_op jit(solution)/shard_map/all_to_all | solution.py:222
  59.2 5.6 %shard_map.88 = (f32[16,48,128]{2,1,0:T(8,128)S(1)}, bf16[1280,64]{1,0:T(8,128)(2,1)S(1)}, bf16[40,1280]{1,0:T(8,128)(2,1)S(1)}, bf16[16,1280]{1,0:T(8,128)(2,1)S(1)}) custom-call(f32[16,128]{1,0:T(8,128)S(1)} %get-tuple-element.31.refs_0_, bf16[16,32,128]{2,1,0:T(8,128)(2,1)S(1)} %all-to-all-done.1.refs_0_.refs_1_, ...), custom_call_target="tpu_custom_call" | custom-call | flops 5368709120 | bytes 1048576 | tf_op jit(solution)/shard_map/pallas_call | solution.py:287
  64.8 1.9 %collective-permute-start.1 = (f32[16,48,128]{2,1,0:T(8,128)S(1)}, f32[16,48,128]{2,1,0:T(8,128)S(1)}, u32[]{:S(2)}, u32[]{:S(2)}) collective-permute-start(f32[16,48,128]{2,1,0:T(8,128)S(1)} %get-tuple-element.39), channel_id=1, source_target_pairs={{0,32},{32,0},{1,33},{33,1},{2,34},{34,2},{3,35},{35,3},{4,36},{36... | collective-permute-start | bytes 1179656 | tf_op jit(solution)/shard_map/ppermute | solution.py:226
  66.7 4.6 %shard_map.89 = f32[16,48,128]{2,1,0:T(8,128)S(1)} custom-call(f32[16,128]{1,0:T(8,128)S(1)} %get-tuple-element.31.refs_0_, bf16[16,48,128]{2,1,0:T(8,128)(2,1)S(1)} %all-to-all-done.refs_0_.refs_1_, bf16[64,2048]{1,0:T(8,128)(2,1)S(1)} %get-tuple-element.32.refs_2_, bf16[64,2048]{1,0:T(8,128)(2,1)S(1)} %get-tuple-element.33.refs_3_, ...), custom_call_target="tpu_custom_call" | custom-call | flops 5368709120 | bytes 1048576 | tf_op jit(solution)/shard_map/pallas_call | solution.py:300
  71.3 0.0 collective-permute-done.1
  71.3 0.7 add_convert_fusion
  72.0 0.0 all-to-all-done.2.parts_ref
  72.0 3.5 %all-to-all-start.3 = ((bf16[16,48,128]{2,1,0:T(8,128)(2,1)}), bf16[16,48,128]{2,1,0:T(8,128)(2,1)S(1)}, u32[]{:S(2)}, u32[]{:S(2)}) async-start(bf16[16,48,128]{2,1,0:T(8,128)(2,1)} %add_convert_fusion), calls=%async_computation.3 | async-start | bytes 393216 | tf_op jit(solution)/shard_map/all_to_all | solution.py:222
  75.6 0.7 shard_map.90
  76.2 8.2 %all-to-all-done.3.refs_0_ = bf16[16,48,128]{2,1,0:T(8,128)(2,1)S(1)} async-done(((bf16[16,48,128]{2,1,0:T(8,128)(2,1)}), bf16[16,48,128]{2,1,0:T(8,128)(2,1)S(1)}, u32[]{:S(2)}, u32[]{:S(2)}) %all-to-all-start.3) | async-done | bytes 196640 | tf_op jit(solution)/shard_map/all_to_all | solution.py:222
  84.4 0.6 shard_map.91
Async XLA Ops:
  2.1 7.1 %copy-start = (bf16[32,80]{1,0:T(8,128)(2,1)S(1)}, bf16[32,80]{1,0:T(8,128)(2,1)}, u32[]{:S(2)}) copy-start(bf16[32,80]{1,0:T(8,128)(2,1)} %feats_ref.1) | copy-start | bytes 15364
  2.1 7.1 %copy-start.1 = (bf16[16,80]{1,0:T(8,128)(2,1)S(1)}, bf16[16,80]{1,0:T(8,128)(2,1)}, u32[]{:S(2)}) copy-start(bf16[16,80]{1,0:T(8,128)(2,1)} %factor_ref.1) | copy-start | bytes 7684
  2.1 15.4 %all-to-all-start = ((bf16[16,48,128]{2,1,0:T(8,128)(2,1)}), bf16[16,48,128]{2,1,0:T(8,128)(2,1)S(1)}, u32[]{:S(2)}, u32[]{:S(2)}) async-start(bf16[16,48,128]{2,1,0:T(8,128)(2,1)} %get-tuple-element.25), calls=%async_computation | async-start | bytes 393216 | tf_op jit(solution)/shard_map/all_to_all | solution.py:222
  17.5 27.7 %all-to-all-start.1 = ((bf16[16,32,128]{2,1,0:T(8,128)(2,1)}), bf16[16,32,128]{2,1,0:T(8,128)(2,1)S(1)}, u32[]{:S(2)}, u32[]{:S(2)}) async-start(bf16[16,32,128]{2,1,0:T(8,128)(2,1)} %shard_map.85), calls=%async_computation.1 | async-start | bytes 262144 | tf_op jit(solution)/shard_map/all_to_all | solution.py:222
  32.7 3.3 %collective-permute-start = (bf16[16,48,128]{2,1,0:T(8,128)(2,1)S(1)}, bf16[16,48,128]{2,1,0:T(8,128)(2,1)S(1)}, u32[]{:S(2)}, u32[]{:S(2)}) collective-permute-start(bf16[16,48,128]{2,1,0:T(8,128)(2,1)S(1)} %all-to-all-done.refs_0_.refs_1_), channel_id=1, source_target_pairs={{0,32},{32,0},{1,33},{33,1},{2,34},{34,2},{3,35},{35,3},{4,36},{36... | collective-permute-start | bytes 589832 | tf_op jit(solution)/shard_map/ppermute | solution.py:226
  54.6 17.5 %all-to-all-start.2 = ((bf16[16,32,128]{2,1,0:T(8,128)(2,1)}), bf16[16,32,128]{2,1,0:T(8,128)(2,1)S(1)}, u32[]{:S(2)}, u32[]{:S(2)}) async-start(bf16[16,32,128]{2,1,0:T(8,128)(2,1)} %shard_map.87), calls=%async_computation.2 | async-start | bytes 262144 | tf_op jit(solution)/shard_map/all_to_all | solution.py:222
  64.8 6.5 %collective-permute-start.1 = (f32[16,48,128]{2,1,0:T(8,128)S(1)}, f32[16,48,128]{2,1,0:T(8,128)S(1)}, u32[]{:S(2)}, u32[]{:S(2)}) collective-permute-start(f32[16,48,128]{2,1,0:T(8,128)S(1)} %get-tuple-element.39), channel_id=1, source_target_pairs={{0,32},{32,0},{1,33},{33,1},{2,34},{34,2},{3,35},{35,3},{4,36},{36... | collective-permute-start | bytes 1179656 | tf_op jit(solution)/shard_map/ppermute | solution.py:226
  72.0 12.4 %all-to-all-start.3 = ((bf16[16,48,128]{2,1,0:T(8,128)(2,1)}), bf16[16,48,128]{2,1,0:T(8,128)(2,1)S(1)}, u32[]{:S(2)}, u32[]{:S(2)}) async-start(bf16[16,48,128]{2,1,0:T(8,128)(2,1)} %add_convert_fusion), calls=%async_computation.3 | async-start | bytes 393216 | tf_op jit(solution)/shard_map/all_to_all | solution.py:222

commit v5 on v4

--- a/solution.py
+++ b/solution.py
@@ -42,26 +42,36 @@
     return block[:, :width], jnp.concatenate([halves[:rank], halves[rank:]], 1)
 
 
-def source_copies_kernel(feats_ref, factor_ref, out_ref):
-    block = pack(feats_ref[...].astype(F32), factor_ref[...].astype(F32)).astype(BF16)
-    for member in range(out_ref.shape[0]):
-        out_ref[member] = block
-
-
-def target_copies_kernel(rank_hbm, feats_hbm, factor_hbm, out_ref, inverse_ref, rank_ref, feats_ref, factor_ref, sems):
-    pairs = [(rank_hbm, rank_ref), (feats_hbm, feats_ref), (factor_hbm, factor_ref)]
+def load_all(pairs, sems):
     loads = [pltpu.make_async_copy(a, b, sems.at[k]) for k, (a, b) in enumerate(pairs)]
     for load in loads:
         load.start()
     for load in loads:
         load.wait()
+
+
+def source_copies_kernel(feats_hbm, factor_hbm, out_ref, feats_ref, factor_ref, sems):
+    load_all([(feats_hbm, feats_ref), (factor_hbm, factor_ref)], sems)
+    block = pack(feats_ref[...].astype(F32), factor_ref[...].astype(F32)).astype(BF16)
+    for member in range(out_ref.shape[0]):
+        out_ref[member] = block
+
+
+def target_block_kernel(rank_hbm, feats_hbm, factor_hbm, out_ref, inverse_ref, rank_ref, feats_ref, factor_ref, sems):
+    load_all([(rank_hbm, rank_ref), (feats_hbm, feats_ref), (factor_hbm, factor_ref)], sems)
     factor = factor_ref[...]
     inverse_g = inverse_column(rank_ref, factor.shape[1])
     inverse_ref[...] = inverse_g
     scaled = (factor.astype(F32) * inverse_g).astype(BF16)
-    block = jnp.concatenate([feats_ref[...], scaled], 0)
+    out_ref[...] = jnp.concatenate([feats_ref[...], scaled], 0)
+
+
+def target_copies_kernel(own_ref, other_ref, out_ref):
+    own = own_ref[...]
+    other = other_ref[...]
     for member in range(out_ref.shape[0]):
-        out_ref[member] = block
+        out_ref[member, 0] = own
+        out_ref[member, 1] = other
 
 
 def three_parts(value):
@@ -120,26 +130,26 @@
     return (x * sum_w[features : features + 1] - sum_w[:features]) * scale
 
 
-def target_prepare_kernel(features, own_ref, other_ref, a_ref, gw_ref, gc_ref, own_bd, own_bp, other_bd, other_bp):
-    count, _, width = own_ref.shape
-    for half, (ref, bd_ref, bp_ref) in enumerate([(own_ref, own_bd, own_bp), (other_ref, other_bd, other_bp)]):
-        for b in range(count):
-            block = ref[b].astype(F32)
-            put_sublanes(
-                pl.ds((half * count + b) * width, width), block[:features], block[features:], a_ref, gw_ref, gc_ref
-            )
-            put_lanes(pl.ds(b * width, width), block[:features], block[features:], bd_ref, bp_ref)
-
-
-def source_pair_kernel(scale, width, src_ref, a_ref, gw_ref, gc_ref, out_ref, x_ref, q_ref, bd_ref, bp_ref, sum_ref):
-    count, features, _ = src_ref.shape
+def source_prepare_kernel(width, src_ref, x_ref, bd_ref, bp_ref, a_ref, gw_ref, gc_ref, q32_ref, gw32_ref, gc32_ref):
     rank = gc_ref.shape[0]
-    for b in range(count):
+    for b in range(src_ref.shape[0]):
         x, q = unpack(src_ref[b].astype(F32), rank, width)
-        x_ref[:, b * width : (b + 1) * width] = x
-        q_ref[:, b * width : (b + 1) * width] = q
+        at = pl.ds(b * width, width)
+        x_ref[:, at] = x
+        q32_ref[:, at] = q
+        put_sublanes(at, x, q, a_ref, gw32_ref, gc32_ref)
+    gw_ref[...] = gw32_ref[...].astype(BF16)
+    gc_ref[...] = gc32_ref[...].astype(BF16)
+    put_lanes(slice(None), x_ref[...], q32_ref[...], bd_ref, bp_ref)
+
+
+def source_pair_kernel(scale, width, tgt_ref, x_ref, bd_ref, bp_ref, out_ref, a_ref, gw_ref, gc_ref, sum_ref):
+    features = x_ref.shape[0]
+    count, _, _, tgt_width = tgt_ref.shape
+    for b in range(2 * count):
+        block = tgt_ref[b // 2, b % 2].astype(F32)
+        put_sublanes(pl.ds(b * tgt_width, tgt_width), block[:features], block[features:], a_ref, gw_ref, gc_ref)
     lanes = x_ref.shape[1]
-    put_lanes(slice(None), x_ref[...], q_ref[...], bd_ref, bp_ref)
     gw = gw_ref[...]
     gc = gc_ref[...]
     step = lanes // 2
@@ -148,14 +158,19 @@
         sum_w, sum_c = pair_sums(a_ref, gw, gc, bd_ref[:, at], bp_ref[:, at], 1024)
         sum_ref[:features, at] = feature_gradient(x_ref[:, at], sum_w, scale)
         sum_ref[features:, at] = sum_c * scale
-    for b in range(count):
+    for b in range(out_ref.shape[0]):
         block = sum_ref[:, b * width : (b + 1) * width]
         out_ref[b] = pack(block[:features], block[features:]).astype(out_ref.dtype)
 
 
-def target_chunks(scale, inverse_ref, from_ref, a_ref, gw, gc, bd_ref, bp_ref, to_ref):
-    count, rows, width = from_ref.shape
-    features = rows - gc.shape[0]
+def target_pair_kernel(scale, half, inverse_ref, tgt_ref, a_ref, gw_ref, gc_ref, out_ref, bd_ref, bp_ref):
+    count, _, rows, width = tgt_ref.shape
+    features = rows - gc_ref.shape[0]
+    for b in range(count):
+        block = tgt_ref[b, half].astype(F32)
+        put_lanes(pl.ds(b * width, width), block[:features], block[features:], bd_ref, bp_ref)
+    gw = gw_ref[...]
+    gc = gc_ref[...]
     factor_scale = inverse_ref[...] * scale
     group = 8
     step = group * width
@@ -165,27 +180,12 @@
         sum_w, sum_c = pair_sums(a_ref, gw, gc, bd_ref[:, at], bp_ref[:, at], a_ref.shape[0] // 2)
         for k in range(group):
             lanes = slice(k * width, (k + 1) * width)
-            x = from_ref[index * group + k][:features].astype(F32)
+            x = tgt_ref[index * group + k, half][:features].astype(F32)
             grad = feature_gradient(x, sum_w[:, lanes], scale)
-            to_ref[index * group + k] = jnp.concatenate([grad, sum_c[:, lanes] * factor_scale], 0)
+            out_ref[index * group + k] = jnp.concatenate([grad, sum_c[:, lanes] * factor_scale], 0)
         return carry
 
     lax.fori_loop(0, count // group, advance, 0)
-
-
-def first_target_kernel(scale, src_width, inverse_ref, src_ref, tgt_ref, bd_ref, bp_ref, out_ref, a_ref, gw_ref, gc_ref, gw32_ref, gc32_ref):
-    src_count = src_ref.shape[0]
-    rank = gc_ref.shape[0]
-    for b in range(src_count):
-        x, q = unpack(src_ref[b].astype(F32), rank, src_width)
-        put_sublanes(pl.ds(b * src_width, src_width), x, q, a_ref, gw32_ref, gc32_ref)
-    gw_ref[...] = gw32_ref[...].astype(BF16)
-    gc_ref[...] = gc32_ref[...].astype(BF16)
-    target_chunks(scale, inverse_ref, tgt_ref, a_ref, gw_ref[...], gc_ref[...], bd_ref, bp_ref, out_ref)
-
-
-def second_target_kernel(scale, inverse_ref, tgt_ref, bd_ref, bp_ref, a_ref, gw_ref, gc_ref, out_ref):
-    target_chunks(scale, inverse_ref, tgt_ref, a_ref, gw_ref[...], gc_ref[...], bd_ref, bp_ref, out_ref)
 
 
 def target_sum_kernel(features, parts_ref, feats_ref, factor_ref):
@@ -222,6 +222,10 @@
     return lax.all_to_all(blocks, axes, 0, 0, tiled=True)
 
 
+def in_hbm(array):
+    return pltpu.with_memory_space_constraint(array, pltpu.HBM)
+
+
 def swap(blocks):
     return lax.ppermute(blocks, CORE, [(0, 1), (1, 0)])
 
@@ -237,37 +241,52 @@
     sources = ring * src_width
     targets = 2 * plane * tgt_width
 
-    tgt_copies, inverse_g = call(
-        target_copies_kernel,
+    src_copies = call(
+        source_copies_kernel,
+        (HBM,) * 2,
+        shape(ring, features, LANES, dtype=BF16),
+        (
+            pltpu.VMEM((features, src_width), BF16),
+            pltpu.VMEM((rank, src_width), BF16),
+            pltpu.SemaphoreType.DMA((2,)),
+        ),
+    )(*map(in_hbm, (src_feats, src_factor)))
+    src_blocks = exchange(src_copies, RING)
+    tgt_own, inverse_g = call(
+        target_block_kernel,
         (HBM,) * 3,
-        (shape(plane, rows, tgt_width, dtype=BF16), shape(rank, tgt_width)),
+        (shape(rows, tgt_width, dtype=BF16), shape(rank, tgt_width)),
         (
             pltpu.SMEM((rank,), F32),
             pltpu.VMEM((features, tgt_width), BF16),
             pltpu.VMEM((rank, tgt_width), BF16),
             pltpu.SemaphoreType.DMA((3,)),
         ),
-    )(*(pltpu.with_memory_space_constraint(array, pltpu.HBM) for array in (rank_weight, tgt_feats, tgt_factor)))
-    src_copies = call(source_copies_kernel, (VMEM, VMEM), shape(ring, features, LANES, dtype=BF16))(
-        src_feats, src_factor
+    )(*map(in_hbm, (rank_weight, tgt_feats, tgt_factor)))
+    tgt_copies = call(target_copies_kernel, (VMEM, VMEM), shape(plane, 2, rows, tgt_width, dtype=BF16))(
+        tgt_own, swap(tgt_own)
     )
-    tgt_own = exchange(tgt_copies, PLANE)
-    tgt_own, src_copies = lax.optimization_barrier((tgt_own, src_copies))
-    src_blocks = exchange(src_copies, RING)
-    tgt_other = swap(tgt_own)
-
-    half = plane * tgt_width
-    a, gw, gc, own_bd, own_bp, other_bd, other_bp = call(
-        lambda *refs: target_prepare_kernel(features, *refs),
-        (VMEM, VMEM),
-        (
-            shape(targets, 64, dtype=BF16),
-            shape(features + 8, targets, dtype=BF16),
-            shape(rank, targets, dtype=BF16),
-        )
-        + (shape(64, half, dtype=BF16),) * 4,
+    src_blocks, tgt_copies = lax.optimization_barrier((src_blocks, tgt_copies))
+    tgt_blocks = exchange(tgt_copies, PLANE)
+
+    x, bd, bp, a, gw, gc = call(
+        lambda *refs: source_prepare_kernel(src_width, *refs),
+        (VMEM,),
+        (
+            shape(features, sources),
+            shape(64, sources, dtype=BF16),
+            shape(64, sources, dtype=BF16),
+            shape(sources, 64, dtype=BF16),
+            shape(features + 8, sources, dtype=BF16),
+            shape(rank, sources, dtype=BF16),
+        ),
+        (
+            pltpu.VMEM((rank, sources), F32),
+            pltpu.VMEM((features + 8, sources), F32),
+            pltpu.VMEM((rank, sources), F32),
+        ),
         flops=1 << 22,
-    )(tgt_own, tgt_other)
+    )(src_blocks)
 
     flops = sources * targets * 2 * 256 * 4
     src_parts = call(
@@ -275,34 +294,26 @@
         (VMEM,) * 4,
         shape(ring, features, LANES, dtype=BF16),
         (
-            pltpu.VMEM((features, sources), F32),
-            pltpu.VMEM((rank, sources), F32),
-            pltpu.VMEM((64, sources), BF16),
-            pltpu.VMEM((64, sources), BF16),
+            pltpu.VMEM((targets, 64), BF16),
+            pltpu.VMEM((features + 8, targets), BF16),
+            pltpu.VMEM((rank, targets), BF16),
             pltpu.VMEM((rows, sources), F32),
         ),
         flops,
-    )(src_blocks, a, gw, gc)
+    )(tgt_blocks, x, bd, bp)
     src_sums = exchange(src_parts, RING)
-    send, src_a, src_gw, src_gc = call(
-        lambda *refs: first_target_kernel(scale, src_width, *refs),
-        (VMEM,) * 5,
-        (
+
+    def target_half(half):
+        return call(
+            lambda *refs: target_pair_kernel(scale, half, *refs),
+            (VMEM,) * 5,
             shape(plane, rows, tgt_width),
-            shape(sources, 64, dtype=BF16),
-            shape(features + 8, sources, dtype=BF16),
-            shape(rank, sources, dtype=BF16),
-        ),
-        (pltpu.VMEM((features + 8, sources), F32), pltpu.VMEM((rank, sources), F32)),
-        flops // 2,
-    )(inverse_g, src_blocks, tgt_other, other_bd, other_bp)
-    received = swap(send)
-    keep = call(
-        lambda *refs: second_target_kernel(scale, *refs),
-        (VMEM,) * 7,
-        shape(plane, rows, tgt_width),
-        flops=flops // 2,
-    )(inverse_g, tgt_own, own_bd, own_bp, src_a, src_gw, src_gc)
+            (pltpu.VMEM((64, targets // 2), BF16), pltpu.VMEM((64, targets // 2), BF16)),
+            flops // 2,
+        )(inverse_g, tgt_blocks, a, gw, gc)
+
+    received = swap(target_half(1))
+    keep = target_half(0)
     src_sums, tgt_half = lax.optimization_barrier((src_sums, (keep + received).astype(BF16)))
     tgt_sums = exchange(tgt_half, PLANE)
 

time: 85.7 us -> 87.4 us (1.020)
  waiting for transfers between devices: 25.8 us -> 27.5 us
    all_to_all x4, waiting for transfers between devices: 24.4 us -> 26.4 us  [exchange(): return lax.all_to_all(blocks, axes, 0, 0, tiled=True)]
    pallas_call x5 -> x6, Pallas kernels: 12.9 us -> 13.2 us  [the longest x2 9.34 us: target_half(): call(lambda *refs: target_pair_kernel(scale, half, *refs), (VMEM,) * 5, s...]
  transfers between devices with their start and end apart: 6 -> 6, of which waited for: 4 -> 5; matrix products, arithmetic and copies ran while one was open for 1% -> 1% of each run, Pallas kernels for 14% -> 14%
where the time goes in v5:
time: 87.4 us; the launch traced here: 86.8 us
  starting transfers between devices  34 us (39%)
  waiting for transfers between devices  27.5 us (31%)
  Pallas kernels  23.8 us (27%)
    all_to_all x4, starting transfers between devices, exchange(): return lax.all_to_all(blocks, axes, 0, 0, tiled=True)  30.2 us
    all_to_all x4, waiting for transfers between devices, exchange(): return lax.all_to_all(blocks, axes, 0, 0, tiled=True)  26.4 us
    pallas_call x2, Pallas kernels, target_half(): call(lambda *refs: target_pair_kernel(scale, half, *refs), (VMEM,) * 5, s...  9.34 us
    pallas_call x1, Pallas kernels, local(): call(lambda *refs: source_pair_kernel(scale, src_width, *refs), (VMEM,) *...  9.31 us
    ppermute x2, starting transfers between devices, swap(): return lax.ppermute(blocks, CORE, [(0, 1), (1, 0)])  3.84 us
  transfers between devices with their start and end apart: 6, of which 5 were waited for; matrix products, arithmetic and copies ran while one was open for 1% of the time, Pallas kernels for 14%

profile of v5, /device:TPU:32, one launch (start us, length us, event | category | flops | bytes accessed | tf_op | source)
XLA Modules:
  0.0 86.8 jit_solution(6029429669349949076)
XLA Ops:
  0.6 1.5 %shard_map.84 = bf16[16,32,128]{2,1,0:T(8,128)(2,1)} custom-call(bf16[32,80]{1,0:T(8,128)(2,1)} %feats_hbm.2, bf16[16,80]{1,0:T(8,128)(2,1)} %factor_hbm.2), custom_call_target="tpu_custom_call" | custom-call | bytes 1048576 | tf_op jit(solution)/shard_map/pallas_call | solution.py:244
  2.1 15.2 %all-to-all-start = ((bf16[16,32,128]{2,1,0:T(8,128)(2,1)}), bf16[16,32,128]{2,1,0:T(8,128)(2,1)S(1)}, u32[]{:S(2)}, u32[]{:S(2)}) async-start(bf16[16,32,128]{2,1,0:T(8,128)(2,1)} %shard_map.84), calls=%async_computation | async-start | bytes 262144 | tf_op jit(solution)/shard_map/all_to_all | solution.py:222
  17.4 0.7 shard_map.85
  18.1 1.9 %collective-permute-start = (bf16[48,128]{1,0:T(8,128)(2,1)S(1)}, bf16[48,128]{1,0:T(8,128)(2,1)S(1)}, u32[]{:S(2)}, u32[]{:S(2)}) collective-permute-start(bf16[48,128]{1,0:T(8,128)(2,1)S(1)} %get-tuple-element.20.own_ref), channel_id=1, source_target_pairs={{0,32},{32,0},{1,33},{33,1},{2,34},{34,2},{3,35},{35,3},{4,36},{36... | collective-permute-start | bytes 36872 | tf_op jit(solution)/shard_map/ppermute | solution.py:230
  20.1 1.1 %collective-permute-done.other_ref = bf16[48,128]{1,0:T(8,128)(2,1)S(1)} collective-permute-done((bf16[48,128]{1,0:T(8,128)(2,1)S(1)}, bf16[48,128]{1,0:T(8,128)(2,1)S(1)}, u32[]{:S(2)}, u32[]{:S(2)}) %collective-permute-start) | collective-permute-done | bytes 12320 | tf_op jit(solution)/shard_map/ppermute | solution.py:230
  21.2 0.8 shard_map.86
  22.0 9.6 %all-to-all-done.refs_0_ = bf16[16,32,128]{2,1,0:T(8,128)(2,1)S(1)} async-done(((bf16[16,32,128]{2,1,0:T(8,128)(2,1)}), bf16[16,32,128]{2,1,0:T(8,128)(2,1)S(1)}, u32[]{:S(2)}, u32[]{:S(2)}) %all-to-all-start) | async-done | bytes 131104 | tf_op jit(solution)/shard_map/all_to_all | solution.py:222
  31.6 7.0 %all-to-all-start.1 = ((bf16[16,2,48,128]{3,2,1,0:T(8,128)(2,1)}), bf16[16,2,48,128]{3,2,1,0:T(8,128)(2,1)S(1)}, u32[]{:S(2)}, u32[]{:S(2)}) async-start(bf16[16,2,48,128]{3,2,1,0:T(8,128)(2,1)} %shard_map.86), calls=%async_computation.1 | async-start | bytes 786432 | tf_op jit(solution)/shard_map/all_to_all | solution.py:222
  38.6 0.8 shard_map.87
  39.5 8.6 %all-to-all-done.1.refs_0_.refs_1_ = bf16[16,2,48,128]{3,2,1,0:T(8,128)(2,1)S(1)} async-done(((bf16[16,2,48,128]{3,2,1,0:T(8,128)(2,1)}), bf16[16,2,48,128]{3,2,1,0:T(8,128)(2,1)S(1)}, u32[]{:S(2)}, u32[]{:S(2)}) %all-to-all-start.1) | async-done | bytes 393248 | tf_op jit(solution)/shard_map/all_to_all | solution.py:222
  48.0 9.3 %shard_map.88 = bf16[16,32,128]{2,1,0:T(8,128)(2,1)} custom-call(bf16[16,2,48,128]{3,2,1,0:T(8,128)(2,1)S(1)} %all-to-all-done.1.refs_0_.refs_1_, f32[32,1280]{1,0:T(8,128)S(1)} %get-tuple-element.23.refs_1_, bf16[64,1280]{1,0:T(8,128)(2,1)S(1)} %get-tuple-element.24.refs_2_, bf16[64,1280]{1,0:T(8,128)(2,1)S(1)} %get-tuple-element.25.refs_3_), custom_call_target="tpu_custom_call" | custom-call | flops 10737418240 | bytes 1048576 | tf_op jit(solution)/shard_map/pallas_call | solution.py:292
  57.3 4.4 %all-to-all-start.2 = ((bf16[16,32,128]{2,1,0:T(8,128)(2,1)}), bf16[16,32,128]{2,1,0:T(8,128)(2,1)S(1)}, u32[]{:S(2)}, u32[]{:S(2)}) async-start(bf16[16,32,128]{2,1,0:T(8,128)(2,1)} %shard_map.88), calls=%async_computation.2 | async-start | bytes 262144 | tf_op jit(solution)/shard_map/all_to_all | solution.py:222
  61.7 4.7 %shard_map.90 = f32[16,48,128]{2,1,0:T(8,128)S(1)} custom-call(f32[16,128]{1,0:T(8,128)S(1)} %get-tuple-element.26.refs_0_, bf16[16,2,48,128]{3,2,1,0:T(8,128)(2,1)S(1)} %all-to-all-done.1.refs_0_.refs_1_, bf16[1280,64]{1,0:T(8,128)(2,1)S(1)} %get-tuple-element.27.refs_2_, bf16[40,1280]{1,0:T(8,128)(2,1)S(1)} %get-tuple-element.28.refs_3_, ...), custom_call_target="tpu_custom_call" | custom-call | flops 5368709120 | bytes 1048576 | tf_op jit(solution)/shard_map/pallas_call | solution.py:307
  66.4 1.9 %collective-permute-start.1 = (f32[16,48,128]{2,1,0:T(8,128)S(1)}, f32[16,48,128]{2,1,0:T(8,128)S(1)}, u32[]{:S(2)}, u32[]{:S(2)}) collective-permute-start(f32[16,48,128]{2,1,0:T(8,128)S(1)} %shard_map.90), channel_id=1, source_target_pairs={{0,32},{32,0},{1,33},{33,1},{2,34},{34,2},{3,35},{35,3},{4,36},{36... | collective-permute-start | bytes 1179656 | tf_op jit(solution)/shard_map/ppermute | solution.py:230
  68.3 4.7 %shard_map.89 = f32[16,48,128]{2,1,0:T(8,128)S(1)} custom-call(f32[16,128]{1,0:T(8,128)S(1)} %get-tuple-element.26.refs_0_, bf16[16,2,48,128]{3,2,1,0:T(8,128)(2,1)S(1)} %all-to-all-done.1.refs_0_.refs_1_, bf16[1280,64]{1,0:T(8,128)(2,1)S(1)} %get-tuple-element.27.refs_2_, bf16[40,1280]{1,0:T(8,128)(2,1)S(1)} %get-tuple-element.28.refs_3_, ...), custom_call_target="tpu_custom_call" | custom-call | flops 5368709120 | bytes 1048576 | tf_op jit(solution)/shard_map/pallas_call | solution.py:307
  73.0 0.0 collective-permute-done.1
  73.0 0.7 add_convert_fusion
  73.7 0.5 all-to-all-done.2.parts_ref
  74.3 3.5 %all-to-all-start.3 = ((bf16[16,48,128]{2,1,0:T(8,128)(2,1)}), bf16[16,48,128]{2,1,0:T(8,128)(2,1)S(1)}, u32[]{:S(2)}, u32[]{:S(2)}) async-start(bf16[16,48,128]{2,1,0:T(8,128)(2,1)} %add_convert_fusion), calls=%async_computation.3 | async-start | bytes 393216 | tf_op jit(solution)/shard_map/all_to_all | solution.py:222
  77.8 0.7 shard_map.91
  78.5 7.7 %all-to-all-done.3.refs_0_ = bf16[16,48,128]{2,1,0:T(8,128)(2,1)S(1)} async-done(((bf16[16,48,128]{2,1,0:T(8,128)(2,1)}), bf16[16,48,128]{2,1,0:T(8,128)(2,1)S(1)}, u32[]{:S(2)}, u32[]{:S(2)}) %all-to-all-start.3) | async-done | bytes 196640 | tf_op jit(solution)/shard_map/all_to_all | solution.py:222
  86.2 0.6 shard_map.92
Async XLA Ops:
  2.1 29.4 %all-to-all-start = ((bf16[16,32,128]{2,1,0:T(8,128)(2,1)}), bf16[16,32,128]{2,1,0:T(8,128)(2,1)S(1)}, u32[]{:S(2)}, u32[]{:S(2)}) async-start(bf16[16,32,128]{2,1,0:T(8,128)(2,1)} %shard_map.84), calls=%async_computation | async-start | bytes 262144 | tf_op jit(solution)/shard_map/all_to_all | solution.py:222
  18.1 3.1 %collective-permute-start = (bf16[48,128]{1,0:T(8,128)(2,1)S(1)}, bf16[48,128]{1,0:T(8,128)(2,1)S(1)}, u32[]{:S(2)}, u32[]{:S(2)}) collective-permute-start(bf16[48,128]{1,0:T(8,128)(2,1)S(1)} %get-tuple-element.20.own_ref), channel_id=1, source_target_pairs={{0,32},{32,0},{1,33},{33,1},{2,34},{34,2},{3,35},{35,3},{4,36},{36... | collective-permute-start | bytes 36872 | tf_op jit(solution)/shard_map/ppermute | solution.py:230
  31.6 16.4 %all-to-all-start.1 = ((bf16[16,2,48,128]{3,2,1,0:T(8,128)(2,1)}), bf16[16,2,48,128]{3,2,1,0:T(8,128)(2,1)S(1)}, u32[]{:S(2)}, u32[]{:S(2)}) async-start(bf16[16,2,48,128]{3,2,1,0:T(8,128)(2,1)} %shard_map.86), calls=%async_computation.1 | async-start | bytes 786432 | tf_op jit(solution)/shard_map/all_to_all | solution.py:222
  57.3 16.9 %all-to-all-start.2 = ((bf16[16,32,128]{2,1,0:T(8,128)(2,1)}), bf16[16,32,128]{2,1,0:T(8,128)(2,1)S(1)}, u32[]{:S(2)}, u32[]{:S(2)}) async-start(bf16[16,32,128]{2,1,0:T(8,128)(2,1)} %shard_map.88), calls=%async_computation.2 | async-start | bytes 262144 | tf_op jit(solution)/shard_map/all_to_all | solution.py:222
  66.4 6.6 %collective-permute-start.1 = (f32[16,48,128]{2,1,0:T(8,128)S(1)}, f32[16,48,128]{2,1,0:T(8,128)S(1)}, u32[]{:S(2)}, u32[]{:S(2)}) collective-permute-start(f32[16,48,128]{2,1,0:T(8,128)S(1)} %shard_map.90), channel_id=1, source_target_pairs={{0,32},{32,0},{1,33},{33,1},{2,34},{34,2},{3,35},{35,3},{4,36},{36... | collective-permute-start | bytes 1179656 | tf_op jit(solution)/shard_map/ppermute | solution.py:230
  74.3 11.9 %all-to-all-start.3 = ((bf16[16,48,128]{2,1,0:T(8,128)(2,1)}), bf16[16,48,128]{2,1,0:T(8,128)(2,1)S(1)}, u32[]{:S(2)}, u32[]{:S(2)}) async-start(bf16[16,48,128]{2,1,0:T(8,128)(2,1)} %add_convert_fusion), calls=%async_computation.3 | async-start | bytes 393216 | tf_op jit(solution)/shard_map/all_to_all | solution.py:222

commit v6 on v4

--- a/solution.py
+++ b/solution.py
@@ -83,22 +83,21 @@
         [-2.0 * x, q] + three_parts(squares(x)) + [ones] * 3 + [jnp.zeros((10, width), F32)], 0
     )
     a_ref[at, :] = stack.T.astype(BF16)
-    gw_ref[:, at] = jnp.concatenate([x, ones, jnp.zeros((7, width), F32)], 0).astype(gw_ref.dtype)
-    gc_ref[:, at] = q.astype(gc_ref.dtype)
-
-
-def put_lanes(at, x, q, bd_ref, bp_ref):
+    gw_ref[:, at] = jnp.concatenate([x, ones, jnp.zeros((7, width), F32)], 0).astype(BF16)
+    gc_ref[:, at] = q.astype(BF16)
+
+
+def lane_operands(x, q):
     features, width = x.shape
     rank = q.shape[0]
-    bd_ref[:, at] = jnp.concatenate(
+    distance = jnp.concatenate(
         [x, jnp.zeros((rank, width), F32), jnp.ones((3, width), F32)]
         + three_parts(squares(x) + 1.0)
         + [jnp.zeros((10, width), F32)],
         0,
-    ).astype(BF16)
-    bp_ref[:, at] = jnp.concatenate(
-        [jnp.zeros((features, width), F32), q, jnp.zeros((16, width), F32)], 0
-    ).astype(BF16)
+    )
+    plan = jnp.concatenate([jnp.zeros((features, width), F32), q, jnp.zeros((16, width), F32)], 0)
+    return distance.astype(BF16), plan.astype(BF16)
 
 
 def pair_sums(a_ref, gw, gc, bd, bp, step):
@@ -128,25 +127,25 @@
             put_sublanes(
                 pl.ds((half * count + b) * width, width), block[:features], block[features:], a_ref, gw_ref, gc_ref
             )
-            put_lanes(pl.ds(b * width, width), block[:features], block[features:], bd_ref, bp_ref)
-
-
-def source_pair_kernel(scale, width, src_ref, a_ref, gw_ref, gc_ref, out_ref, x_ref, q_ref, bd_ref, bp_ref, sum_ref):
+            lanes = pl.ds(b * width, width)
+            bd_ref[:, lanes], bp_ref[:, lanes] = lane_operands(block[:features], block[features:])
+
+
+def source_pair_kernel(scale, width, src_ref, a_ref, gw_ref, gc_ref, out_ref, all_ref, bd_ref, bp_ref, sum_ref):
     count, features, _ = src_ref.shape
     rank = gc_ref.shape[0]
     for b in range(count):
-        x, q = unpack(src_ref[b].astype(F32), rank, width)
-        x_ref[:, b * width : (b + 1) * width] = x
-        q_ref[:, b * width : (b + 1) * width] = q
-    lanes = x_ref.shape[1]
-    put_lanes(slice(None), x_ref[...], q_ref[...], bd_ref, bp_ref)
+        lanes = slice(b * width, (b + 1) * width)
+        all_ref[:features, lanes], all_ref[features:, lanes] = unpack(src_ref[b].astype(F32), rank, width)
+    bd_ref[...], bp_ref[...] = lane_operands(all_ref[:features], all_ref[features:])
     gw = gw_ref[...]
     gc = gc_ref[...]
-    step = lanes // 2
-    for start in range(0, lanes, step):
+    total = all_ref.shape[1]
+    step = total // 2
+    for start in range(0, total, step):
         at = slice(start, start + step)
         sum_w, sum_c = pair_sums(a_ref, gw, gc, bd_ref[:, at], bp_ref[:, at], 1024)
-        sum_ref[:features, at] = feature_gradient(x_ref[:, at], sum_w, scale)
+        sum_ref[:features, at] = feature_gradient(all_ref[:features, at], sum_w, scale)
         sum_ref[features:, at] = sum_c * scale
     for b in range(count):
         block = sum_ref[:, b * width : (b + 1) * width]
@@ -173,19 +172,17 @@
     lax.fori_loop(0, count // group, advance, 0)
 
 
-def first_target_kernel(scale, src_width, inverse_ref, src_ref, tgt_ref, bd_ref, bp_ref, out_ref, a_ref, gw_ref, gc_ref, gw32_ref, gc32_ref):
-    src_count = src_ref.shape[0]
-    rank = gc_ref.shape[0]
-    for b in range(src_count):
-        x, q = unpack(src_ref[b].astype(F32), rank, src_width)
-        put_sublanes(pl.ds(b * src_width, src_width), x, q, a_ref, gw32_ref, gc32_ref)
-    gw_ref[...] = gw32_ref[...].astype(BF16)
-    gc_ref[...] = gc32_ref[...].astype(BF16)
+def first_target_kernel(scale, features, inverse_ref, src_ref, tgt_ref, bd_ref, bp_ref, out_ref, a_ref, gw_ref, gc_ref):
+    put_sublanes(slice(None), src_ref[:features], src_ref[features:], a_ref, gw_ref, gc_ref)
     target_chunks(scale, inverse_ref, tgt_ref, a_ref, gw_ref[...], gc_ref[...], bd_ref, bp_ref, out_ref)
 
 
 def second_target_kernel(scale, inverse_ref, tgt_ref, bd_ref, bp_ref, a_ref, gw_ref, gc_ref, out_ref):
     target_chunks(scale, inverse_ref, tgt_ref, a_ref, gw_ref[...], gc_ref[...], bd_ref, bp_ref, out_ref)
+
+
+def add_kernel(a_ref, b_ref, out_ref):
+    out_ref[...] = (a_ref[...] + b_ref[...]).astype(out_ref.dtype)
 
 
 def target_sum_kernel(features, parts_ref, feats_ref, factor_ref):
@@ -270,13 +267,11 @@
     )(tgt_own, tgt_other)
 
     flops = sources * targets * 2 * 256 * 4
-    src_parts = call(
+    src_parts, src_all = call(
         lambda *refs: source_pair_kernel(scale, src_width, *refs),
         (VMEM,) * 4,
-        shape(ring, features, LANES, dtype=BF16),
+        (shape(ring, features, LANES, dtype=BF16), shape(rows, sources)),
         (
-            pltpu.VMEM((features, sources), F32),
-            pltpu.VMEM((rank, sources), F32),
             pltpu.VMEM((64, sources), BF16),
             pltpu.VMEM((64, sources), BF16),
             pltpu.VMEM((rows, sources), F32),
@@ -285,7 +280,7 @@
     )(src_blocks, a, gw, gc)
     src_sums = exchange(src_parts, RING)
     send, src_a, src_gw, src_gc = call(
-        lambda *refs: first_target_kernel(scale, src_width, *refs),
+        lambda *refs: first_target_kernel(scale, features, *refs),
         (VMEM,) * 5,
         (
             shape(plane, rows, tgt_width),
@@ -293,9 +288,8 @@
             shape(features + 8, sources, dtype=BF16),
             shape(rank, sources, dtype=BF16),
         ),
-        (pltpu.VMEM((features + 8, sources), F32), pltpu.VMEM((rank, sources), F32)),
-        flops // 2,
-    )(inverse_g, src_blocks, tgt_other, other_bd, other_bp)
+        flops=flops // 2,
+    )(inverse_g, src_all, tgt_other, other_bd, other_bp)
     received = swap(send)
     keep = call(
         lambda *refs: second_target_kernel(scale, *refs),
@@ -303,7 +297,8 @@
         shape(plane, rows, tgt_width),
         flops=flops // 2,
     )(inverse_g, tgt_own, own_bd, own_bp, src_a, src_gw, src_gc)
-    src_sums, tgt_half = lax.optimization_barrier((src_sums, (keep + received).astype(BF16)))
+    tgt_half = call(add_kernel, (VMEM, VMEM), shape(plane, rows, tgt_width, dtype=BF16))(keep, received)
+    src_sums, tgt_half = lax.optimization_barrier((src_sums, tgt_half))
     tgt_sums = exchange(tgt_half, PLANE)
 
     grad_x, grad_q = call(source_sum_kernel, (VMEM,), (shape(features, src_width), shape(rank, src_width)))(src_sums)

time: 85.7 us -> 85.4 us (level)
  the two profiles are of different devices: /device:TPU:32 before, /device:TPU:2 now
where the time goes in v6:
time: 85.4 us; the launch traced here: 84.7 us
  starting transfers between devices  34.7 us (41%)
  waiting for transfers between devices  25.9 us (30%)
  Pallas kernels  23.4 us (27%)
    all_to_all x4, starting transfers between devices, exchange(): return lax.all_to_all(blocks, axes, 0, 0, tiled=True)  30.8 us
    all_to_all x4, waiting for transfers between devices, exchange(): return lax.all_to_all(blocks, axes, 0, 0, tiled=True)  24.5 us
    pallas_call x1, Pallas kernels, local(): call(lambda *refs: source_pair_kernel(scale, src_width, *refs), (VMEM,) *...  9.33 us
    pallas_call x1, Pallas kernels, local(): call(lambda *refs: first_target_kernel(scale, features, *refs), (VMEM,) *...  4.73 us
    pallas_call x1, Pallas kernels, local(): call(lambda *refs: second_target_kernel(scale, *refs), (VMEM,) * 7, shape...  4.55 us
    ppermute x2, starting transfers between devices, swap(): return lax.ppermute(blocks, CORE, [(0, 1), (1, 0)])  3.84 us
  transfers between devices with their start and end apart: 6, of which 5 were waited for; matrix products, arithmetic and copies ran while one was open for 0% of the time, Pallas kernels for 14%

profile of v6, /device:TPU:2, one launch (start us, length us, event | category | flops | bytes accessed | tf_op | source)
XLA Modules:
  0.0 84.7 jit_solution(6610714651477852250)
XLA Ops:
  0.6 1.4 %shard_map.84 = (bf16[16,48,128]{2,1,0:T(8,128)(2,1)}, f32[16,128]{1,0:T(8,128)S(1)}) custom-call(f32[16]{0:T(128)} %rank_hbm.1, bf16[32,128]{1,0:T(8,128)(2,1)} %feats_hbm.1, bf16[16,128]{1,0:T(8,128)(2,1)} %factor_hbm.1), custom_call_target="tpu_custom_call" | custom-call | bytes 1048576 | tf_op jit(solution)/shard_map/pallas_call | solution.py:237
  2.1 0.0 copy-start
  2.1 0.0 copy-start.1
  2.1 9.2 %all-to-all-start = ((bf16[16,48,128]{2,1,0:T(8,128)(2,1)}), bf16[16,48,128]{2,1,0:T(8,128)(2,1)S(1)}, u32[]{:S(2)}, u32[]{:S(2)}) async-start(bf16[16,48,128]{2,1,0:T(8,128)(2,1)} %get-tuple-element.27), calls=%async_computation | async-start | bytes 393216 | tf_op jit(solution)/shard_map/all_to_all | solution.py:219
  11.3 0.0 copy-done
  11.3 0.0 copy-done.1
  11.3 0.8 shard_map.85
  12.1 6.3 %all-to-all-done.refs_0_.refs_1_ = bf16[16,48,128]{2,1,0:T(8,128)(2,1)S(1)} async-done(((bf16[16,48,128]{2,1,0:T(8,128)(2,1)}), bf16[16,48,128]{2,1,0:T(8,128)(2,1)S(1)}, u32[]{:S(2)}, u32[]{:S(2)}) %all-to-all-start) | async-done | bytes 196640 | tf_op jit(solution)/shard_map/all_to_all | solution.py:219
  18.4 13.4 %all-to-all-start.1 = ((bf16[16,32,128]{2,1,0:T(8,128)(2,1)}), bf16[16,32,128]{2,1,0:T(8,128)(2,1)S(1)}, u32[]{:S(2)}, u32[]{:S(2)}) async-start(bf16[16,32,128]{2,1,0:T(8,128)(2,1)} %shard_map.85), calls=%async_computation.1 | async-start | bytes 262144 | tf_op jit(solution)/shard_map/all_to_all | solution.py:219
  31.8 1.9 %collective-permute-start = (bf16[16,48,128]{2,1,0:T(8,128)(2,1)S(1)}, bf16[16,48,128]{2,1,0:T(8,128)(2,1)S(1)}, u32[]{:S(2)}, u32[]{:S(2)}) collective-permute-start(bf16[16,48,128]{2,1,0:T(8,128)(2,1)S(1)} %all-to-all-done.refs_0_.refs_1_), channel_id=1, source_target_pairs={{0,32},{32,0},{1,33},{33,1},{2,34},{34,2},{3,35},{35,3},{4,36},{36... | collective-permute-start | bytes 589832 | tf_op jit(solution)/shard_map/ppermute | solution.py:223
  33.7 1.4 %collective-permute-done.refs_1_.refs_2_ = bf16[16,48,128]{2,1,0:T(8,128)(2,1)S(1)} collective-permute-done((bf16[16,48,128]{2,1,0:T(8,128)(2,1)S(1)}, bf16[16,48,128]{2,1,0:T(8,128)(2,1)S(1)}, u32[]{:S(2)}, u32[]{:S(2)}) %collective-permute-start) | collective-permute-done | bytes 196640 | tf_op jit(solution)/shard_map/ppermute | solution.py:223
  35.1 0.5 shard_map.86
  35.6 10.1 %all-to-all-done.1.refs_0_ = bf16[16,32,128]{2,1,0:T(8,128)(2,1)S(1)} async-done(((bf16[16,32,128]{2,1,0:T(8,128)(2,1)}), bf16[16,32,128]{2,1,0:T(8,128)(2,1)S(1)}, u32[]{:S(2)}, u32[]{:S(2)}) %all-to-all-start.1) | async-done | bytes 131104 | tf_op jit(solution)/shard_map/all_to_all | solution.py:219
  45.7 9.3 %shard_map.87 = (bf16[16,32,128]{2,1,0:T(8,128)(2,1)}, f32[48,1280]{1,0:T(8,128)S(1)}) custom-call(bf16[16,32,128]{2,1,0:T(8,128)(2,1)S(1)} %all-to-all-done.1.refs_0_, bf16[4096,64]{1,0:T(8,128)(2,1)S(1)} %get-tuple-element.30.refs_1_, bf16[40,4096]{1,0:T(8,128)(2,1)S(1)} %get-tuple-element.31.refs_2_, bf16[16,4096]{1,0:T(8,128)(2,1)S(1)} %get-tuple-element.32.refs_3_), custom_call_target="tpu_custom_call" | custom-call | flops 10737418240 | bytes 1048576 | tf_op jit(solution)/shard_map/pallas_call | solution.py:270
  55.1 3.7 %all-to-all-start.2 = ((bf16[16,32,128]{2,1,0:T(8,128)(2,1)}), bf16[16,32,128]{2,1,0:T(8,128)(2,1)S(1)}, u32[]{:S(2)}, u32[]{:S(2)}) async-start(bf16[16,32,128]{2,1,0:T(8,128)(2,1)} %get-tuple-element.33), calls=%async_computation.2 | async-start | bytes 262144 | tf_op jit(solution)/shard_map/all_to_all | solution.py:219
  58.8 4.7 %shard_map.88 = (f32[16,48,128]{2,1,0:T(8,128)S(1)}, bf16[1280,64]{1,0:T(8,128)(2,1)S(1)}, bf16[40,1280]{1,0:T(8,128)(2,1)S(1)}, bf16[16,1280]{1,0:T(8,128)(2,1)S(1)}) custom-call(f32[16,128]{1,0:T(8,128)S(1)} %get-tuple-element.34.refs_0_, f32[48,1280]{1,0:T(8,128)S(1)} %get-tuple-element.37.refs_1_, ...), custom_call_target="tpu_custom_call" | custom-call | flops 5368709120 | bytes 1048576 | tf_op jit(solution)/shard_map/pallas_call | solution.py:282
  63.5 1.9 %collective-permute-start.1 = (f32[16,48,128]{2,1,0:T(8,128)S(1)}, f32[16,48,128]{2,1,0:T(8,128)S(1)}, u32[]{:S(2)}, u32[]{:S(2)}) collective-permute-start(f32[16,48,128]{2,1,0:T(8,128)S(1)} %get-tuple-element.43), channel_id=1, source_target_pairs={{0,32},{32,0},{1,33},{33,1},{2,34},{34,2},{3,35},{35,3},{4,36},{36... | collective-permute-start | bytes 1179656 | tf_op jit(solution)/shard_map/ppermute | solution.py:223
  65.4 4.6 %shard_map.89.a_ref = f32[16,48,128]{2,1,0:T(8,128)S(1)} custom-call(f32[16,128]{1,0:T(8,128)S(1)} %get-tuple-element.34.refs_0_, bf16[16,48,128]{2,1,0:T(8,128)(2,1)S(1)} %all-to-all-done.refs_0_.refs_1_, bf16[64,2048]{1,0:T(8,128)(2,1)S(1)} %get-tuple-element.35.refs_2_, bf16[64,2048]{1,0:T(8,128)(2,1)S(1)} %get-tuple-element.36.refs_3_, ...), custom_call_target="tpu_custom_call" | custom-call | flops 5368709120 | bytes 1048576 | tf_op jit(solution)/shard_map/pallas_call | solution.py:294
  70.0 0.0 collective-permute-done.1.b_ref
  70.0 0.7 shard_map.90
  70.7 1.8 %all-to-all-done.2.parts_ref = bf16[16,32,128]{2,1,0:T(8,128)(2,1)S(1)} async-done(((bf16[16,32,128]{2,1,0:T(8,128)(2,1)}), bf16[16,32,128]{2,1,0:T(8,128)(2,1)S(1)}, u32[]{:S(2)}, u32[]{:S(2)}) %all-to-all-start.2) | async-done | bytes 131104 | tf_op jit(solution)/shard_map/all_to_all | solution.py:219
  72.5 4.6 %all-to-all-start.3 = ((bf16[16,48,128]{2,1,0:T(8,128)(2,1)}), bf16[16,48,128]{2,1,0:T(8,128)(2,1)S(1)}, u32[]{:S(2)}, u32[]{:S(2)}) async-start(bf16[16,48,128]{2,1,0:T(8,128)(2,1)} %shard_map.90), calls=%async_computation.3 | async-start | bytes 393216 | tf_op jit(solution)/shard_map/all_to_all | solution.py:219
  77.0 0.7 shard_map.91
  77.7 6.4 %all-to-all-done.3.refs_0_ = bf16[16,48,128]{2,1,0:T(8,128)(2,1)S(1)} async-done(((bf16[16,48,128]{2,1,0:T(8,128)(2,1)}), bf16[16,48,128]{2,1,0:T(8,128)(2,1)S(1)}, u32[]{:S(2)}, u32[]{:S(2)}) %all-to-all-start.3) | async-done | bytes 196640 | tf_op jit(solution)/shard_map/all_to_all | solution.py:219
  84.1 0.6 shard_map.92
Async XLA Ops:
  2.1 9.3 %copy-start = (bf16[32,80]{1,0:T(8,128)(2,1)S(1)}, bf16[32,80]{1,0:T(8,128)(2,1)}, u32[]{:S(2)}) copy-start(bf16[32,80]{1,0:T(8,128)(2,1)} %feats_ref.1) | copy-start | bytes 15364
  2.1 9.2 %copy-start.1 = (bf16[16,80]{1,0:T(8,128)(2,1)S(1)}, bf16[16,80]{1,0:T(8,128)(2,1)}, u32[]{:S(2)}) copy-start(bf16[16,80]{1,0:T(8,128)(2,1)} %factor_ref.1) | copy-start | bytes 7684
  2.1 16.3 %all-to-all-start = ((bf16[16,48,128]{2,1,0:T(8,128)(2,1)}), bf16[16,48,128]{2,1,0:T(8,128)(2,1)S(1)}, u32[]{:S(2)}, u32[]{:S(2)}) async-start(bf16[16,48,128]{2,1,0:T(8,128)(2,1)} %get-tuple-element.27), calls=%async_computation | async-start | bytes 393216 | tf_op jit(solution)/shard_map/all_to_all | solution.py:219
  18.4 27.3 %all-to-all-start.1 = ((bf16[16,32,128]{2,1,0:T(8,128)(2,1)}), bf16[16,32,128]{2,1,0:T(8,128)(2,1)S(1)}, u32[]{:S(2)}, u32[]{:S(2)}) async-start(bf16[16,32,128]{2,1,0:T(8,128)(2,1)} %shard_map.85), calls=%async_computation.1 | async-start | bytes 262144 | tf_op jit(solution)/shard_map/all_to_all | solution.py:219
  31.8 3.3 %collective-permute-start = (bf16[16,48,128]{2,1,0:T(8,128)(2,1)S(1)}, bf16[16,48,128]{2,1,0:T(8,128)(2,1)S(1)}, u32[]{:S(2)}, u32[]{:S(2)}) collective-permute-start(bf16[16,48,128]{2,1,0:T(8,128)(2,1)S(1)} %all-to-all-done.refs_0_.refs_1_), channel_id=1, source_target_pairs={{0,32},{32,0},{1,33},{33,1},{2,34},{34,2},{3,35},{35,3},{4,36},{36... | collective-permute-start | bytes 589832 | tf_op jit(solution)/shard_map/ppermute | solution.py:223
  55.1 17.4 %all-to-all-start.2 = ((bf16[16,32,128]{2,1,0:T(8,128)(2,1)}), bf16[16,32,128]{2,1,0:T(8,128)(2,1)S(1)}, u32[]{:S(2)}, u32[]{:S(2)}) async-start(bf16[16,32,128]{2,1,0:T(8,128)(2,1)} %get-tuple-element.33), calls=%async_computation.2 | async-start | bytes 262144 | tf_op jit(solution)/shard_map/all_to_all | solution.py:219
  63.5 6.5 %collective-permute-start.1 = (f32[16,48,128]{2,1,0:T(8,128)S(1)}, f32[16,48,128]{2,1,0:T(8,128)S(1)}, u32[]{:S(2)}, u32[]{:S(2)}) collective-permute-start(f32[16,48,128]{2,1,0:T(8,128)S(1)} %get-tuple-element.43), channel_id=1, source_target_pairs={{0,32},{32,0},{1,33},{33,1},{2,34},{34,2},{3,35},{35,3},{4,36},{36... | collective-permute-start | bytes 1179656 | tf_op jit(solution)/shard_map/ppermute | solution.py:223
  72.5 11.6 %all-to-all-start.3 = ((bf16[16,48,128]{2,1,0:T(8,128)(2,1)}), bf16[16,48,128]{2,1,0:T(8,128)(2,1)S(1)}, u32[]{:S(2)}, u32[]{:S(2)}) async-start(bf16[16,48,128]{2,1,0:T(8,128)(2,1)} %shard_map.90), calls=%async_computation.3 | async-start | bytes 393216 | tf_op jit(solution)/shard_map/all_to_all | solution.py:219

commit v7 on v6

--- a/solution.py
+++ b/solution.py
@@ -42,26 +42,29 @@
     return block[:, :width], jnp.concatenate([halves[:rank], halves[rank:]], 1)
 
 
-def source_copies_kernel(feats_ref, factor_ref, out_ref):
-    block = pack(feats_ref[...].astype(F32), factor_ref[...].astype(F32)).astype(BF16)
-    for member in range(out_ref.shape[0]):
-        out_ref[member] = block
-
-
-def target_copies_kernel(rank_hbm, feats_hbm, factor_hbm, out_ref, inverse_ref, rank_ref, feats_ref, factor_ref, sems):
-    pairs = [(rank_hbm, rank_ref), (feats_hbm, feats_ref), (factor_hbm, factor_ref)]
+def copies_kernel(rank_hbm, tgt_hbm, tgt_factor_hbm, src_hbm, src_factor_hbm, tgt_out, src_out, inverse_ref, rank_ref, tgt_ref, tgt_factor_ref, src_ref, src_factor_ref, sems):
+    pairs = [
+        (rank_hbm, rank_ref),
+        (tgt_hbm, tgt_ref),
+        (tgt_factor_hbm, tgt_factor_ref),
+        (src_hbm, src_ref),
+        (src_factor_hbm, src_factor_ref),
+    ]
     loads = [pltpu.make_async_copy(a, b, sems.at[k]) for k, (a, b) in enumerate(pairs)]
     for load in loads:
         load.start()
     for load in loads:
         load.wait()
-    factor = factor_ref[...]
+    factor = tgt_factor_ref[...]
     inverse_g = inverse_column(rank_ref, factor.shape[1])
     inverse_ref[...] = inverse_g
     scaled = (factor.astype(F32) * inverse_g).astype(BF16)
-    block = jnp.concatenate([feats_ref[...], scaled], 0)
-    for member in range(out_ref.shape[0]):
-        out_ref[member] = block
+    tgt_block = jnp.concatenate([tgt_ref[...], scaled], 0)
+    for member in range(tgt_out.shape[0]):
+        tgt_out[member] = tgt_block
+    src_block = pack(src_ref[...].astype(F32), src_factor_ref[...].astype(F32)).astype(BF16)
+    for member in range(src_out.shape[0]):
+        src_out[member] = src_block
 
 
 def three_parts(value):
@@ -185,17 +188,12 @@
     out_ref[...] = (a_ref[...] + b_ref[...]).astype(out_ref.dtype)
 
 
-def target_sum_kernel(features, parts_ref, feats_ref, factor_ref):
-    total = jnp.sum(parts_ref[...].astype(F32), 0)
-    feats_ref[...] = total[:features]
-    factor_ref[...] = total[features:]
-
-
-def source_sum_kernel(parts_ref, feats_ref, factor_ref):
-    rank, width = factor_ref.shape
-    feats, factor = unpack(jnp.sum(parts_ref[...].astype(F32), 0), rank, width)
-    feats_ref[...] = feats
-    factor_ref[...] = factor
+def sums_kernel(src_parts_ref, tgt_parts_ref, src_feats, src_factor, tgt_feats, tgt_factor):
+    rank, width = src_factor.shape
+    src_feats[...], src_factor[...] = unpack(jnp.sum(src_parts_ref[...].astype(F32), 0), rank, width)
+    total = jnp.sum(tgt_parts_ref[...].astype(F32), 0)
+    tgt_feats[...] = total[:-rank]
+    tgt_factor[...] = total[-rank:]
 
 
 def call(kernel, specs, outs, scratch=(), flops=0):
@@ -234,19 +232,27 @@
     sources = ring * src_width
     targets = 2 * plane * tgt_width
 
-    tgt_copies, inverse_g = call(
-        target_copies_kernel,
-        (HBM,) * 3,
-        (shape(plane, rows, tgt_width, dtype=BF16), shape(rank, tgt_width)),
+    tgt_copies, src_copies, inverse_g = call(
+        copies_kernel,
+        (HBM,) * 5,
+        (
+            shape(plane, rows, tgt_width, dtype=BF16),
+            shape(ring, features, LANES, dtype=BF16),
+            shape(rank, tgt_width),
+        ),
         (
             pltpu.SMEM((rank,), F32),
             pltpu.VMEM((features, tgt_width), BF16),
             pltpu.VMEM((rank, tgt_width), BF16),
-            pltpu.SemaphoreType.DMA((3,)),
-        ),
-    )(*(pltpu.with_memory_space_constraint(array, pltpu.HBM) for array in (rank_weight, tgt_feats, tgt_factor)))
-    src_copies = call(source_copies_kernel, (VMEM, VMEM), shape(ring, features, LANES, dtype=BF16))(
-        src_feats, src_factor
+            pltpu.VMEM((features, src_width), BF16),
+            pltpu.VMEM((rank, src_width), BF16),
+            pltpu.SemaphoreType.DMA((5,)),
+        ),
+    )(
+        *(
+            pltpu.with_memory_space_constraint(array, pltpu.HBM)
+            for array in (rank_weight, tgt_feats, tgt_factor, src_feats, src_factor)
+        )
     )
     tgt_own = exchange(tgt_copies, PLANE)
     tgt_own, src_copies = lax.optimization_barrier((tgt_own, src_copies))
@@ -301,11 +307,16 @@
     src_sums, tgt_half = lax.optimization_barrier((src_sums, tgt_half))
     tgt_sums = exchange(tgt_half, PLANE)
 
-    grad_x, grad_q = call(source_sum_kernel, (VMEM,), (shape(features, src_width), shape(rank, src_width)))(src_sums)
-    grad_y, grad_r = call(
-        lambda *refs: target_sum_kernel(features, *refs), (VMEM,), (shape(features, tgt_width), shape(rank, tgt_width))
-    )(tgt_sums)
-    return grad_x, grad_q, grad_y, grad_r
+    return call(
+        sums_kernel,
+        (VMEM, VMEM),
+        (
+            shape(features, src_width),
+            shape(rank, src_width),
+            shape(features, tgt_width),
+            shape(rank, tgt_width),
+        ),
+    )(src_sums, tgt_sums)
 
 
 def solution(mesh):

time: 85.4 us -> 84.9 us (level)
  blocking collectives: 0 us -> 26.7 us
  starting transfers between devices: 34.7 us -> 21.6 us
  waiting for transfers between devices: 25.9 us -> 14 us
  Pallas kernels: 23.4 us -> 21.4 us
    all_to_all x0 -> x2, blocking collectives: none -> 26.7 us  [exchange(): return lax.all_to_all(blocks, axes, 0, 0, tiled=True)]
    all_to_all x4 -> x2, starting transfers between devices: 30.8 us -> 17.7 us  [exchange(): return lax.all_to_all(blocks, axes, 0, 0, tiled=True)]
    all_to_all x4 -> x2, waiting for transfers between devices: 24.5 us -> 12.6 us  [exchange(): return lax.all_to_all(blocks, axes, 0, 0, tiled=True)]
    pallas_call x4 -> x2, Pallas kernels: 3.54 us -> 2.28 us  [the longest x1 1.57 us: local(): call(copies_kernel, (HBM,) * 5, (shape(plane, rows, tgt_width, dtype=BF16...]
  transfers between devices with their start and end apart: 6 -> 4, of which waited for: 5 -> 3; matrix products, arithmetic and copies ran while one was open for 0% -> 0% of each run, Pallas kernels for 14% -> 12%
where the time goes in v7:
time: 84.9 us; the launch traced here: 84.4 us
  blocking collectives  26.7 us (31%)
  starting transfers between devices  21.6 us (25%)
  Pallas kernels  21.4 us (25%)
  waiting for transfers between devices  14 us (16%)
    all_to_all x2, blocking collectives, exchange(): return lax.all_to_all(blocks, axes, 0, 0, tiled=True)  26.7 us
    all_to_all x2, starting transfers between devices, exchange(): return lax.all_to_all(blocks, axes, 0, 0, tiled=True)  17.7 us
    all_to_all x2, waiting for transfers between devices, exchange(): return lax.all_to_all(blocks, axes, 0, 0, tiled=True)  12.6 us
    pallas_call x1, Pallas kernels, local(): call(lambda *refs: source_pair_kernel(scale, src_width, *refs), (VMEM,) *...  9.33 us
    pallas_call x1, Pallas kernels, local(): call(lambda *refs: first_target_kernel(scale, features, *refs), (VMEM,) *...  4.72 us
    pallas_call x1, Pallas kernels, local(): call(lambda *refs: second_target_kernel(scale, *refs), (VMEM,) * 7, shape...  4.55 us
    ppermute x2, starting transfers between devices, swap(): return lax.ppermute(blocks, CORE, [(0, 1), (1, 0)])  3.84 us
  transfers between devices with their start and end apart: 4, of which 3 were waited for; matrix products, arithmetic and copies ran while one was open for 0% of the time, Pallas kernels for 12%

profile of v7, /device:TPU:2, one launch (start us, length us, event | category | flops | bytes accessed | tf_op | source)
XLA Modules:
  0.0 84.4 jit_solution(12796965064771968111)
XLA Ops:
  0.6 1.6 %shard_map.84 = (bf16[16,48,128]{2,1,0:T(8,128)(2,1)S(1)}, bf16[16,32,128]{2,1,0:T(8,128)(2,1)}, f32[16,128]{1,0:T(8,128)S(1)}) custom-call(f32[16]{0:T(128)} %rank_hbm.1, bf16[32,128]{1,0:T(8,128)(2,1)} %tgt_hbm.1, bf16[16,128]{1,0:T(8,128)(2,1)} %tgt_factor_hbm.1, bf16[32,80]{1,0:T(8,128)(2,1)} %src_hbm.1, bf16[16,80]{1,0:T(8,128)(2,1)} %src_factor_hbm.1), custom_call_target="tpu_custom_call" | custom-call | bytes 1048576 | tf_op jit(solution)/shard_map/pallas_call | solution.py:235
  2.2 15.4 %all_to_all.20.refs_0_.refs_1_ = bf16[16,48,128]{2,1,0:T(8,128)(2,1)S(1)} all-to-all(bf16[16,48,128]{2,1,0:T(8,128)(2,1)S(1)} %get-tuple-element.24), channel_id=1, replica_groups=mesh['zl'=8,'core'=2,'zh'=2,'y'=4,'x'=4] {'y','x'}, dimensions={0} | all-to-all | bytes 393216 | tf_op jit(solution)/shard_map/all_to_all | solution.py:217
  17.6 14.1 %all-to-all-start.1 = ((bf16[16,32,128]{2,1,0:T(8,128)(2,1)}), bf16[16,32,128]{2,1,0:T(8,128)(2,1)S(1)}, u32[]{:S(2)}, u32[]{:S(2)}) async-start(bf16[16,32,128]{2,1,0:T(8,128)(2,1)} %get-tuple-element.26), calls=%async_computation.1 | async-start | bytes 262144 | tf_op jit(solution)/shard_map/all_to_all | solution.py:217
  31.7 1.9 %collective-permute-start = (bf16[16,48,128]{2,1,0:T(8,128)(2,1)S(1)}, bf16[16,48,128]{2,1,0:T(8,128)(2,1)S(1)}, u32[]{:S(2)}, u32[]{:S(2)}) collective-permute-start(bf16[16,48,128]{2,1,0:T(8,128)(2,1)S(1)} %all_to_all.20.refs_0_.refs_1_), channel_id=1, source_target_pairs={{0,32},{32,0},{1,33},{33,1},{2,34},{34,2},{3,35},{35,3},{4,36},{36... | collective-permute-start | bytes 589832 | tf_op jit(solution)/shard_map/ppermute | solution.py:221
  33.6 1.4 %collective-permute-done.refs_1_.refs_2_ = bf16[16,48,128]{2,1,0:T(8,128)(2,1)S(1)} collective-permute-done((bf16[16,48,128]{2,1,0:T(8,128)(2,1)S(1)}, bf16[16,48,128]{2,1,0:T(8,128)(2,1)S(1)}, u32[]{:S(2)}, u32[]{:S(2)}) %collective-permute-start) | collective-permute-done | bytes 196640 | tf_op jit(solution)/shard_map/ppermute | solution.py:221
  35.0 0.5 shard_map.85
  35.5 10.1 %all-to-all-done.1.refs_0_ = bf16[16,32,128]{2,1,0:T(8,128)(2,1)S(1)} async-done(((bf16[16,32,128]{2,1,0:T(8,128)(2,1)}), bf16[16,32,128]{2,1,0:T(8,128)(2,1)S(1)}, u32[]{:S(2)}, u32[]{:S(2)}) %all-to-all-start.1) | async-done | bytes 131104 | tf_op jit(solution)/shard_map/all_to_all | solution.py:217
  45.6 9.3 %shard_map.86 = (bf16[16,32,128]{2,1,0:T(8,128)(2,1)}, f32[48,1280]{1,0:T(8,128)S(1)}) custom-call(bf16[16,32,128]{2,1,0:T(8,128)(2,1)S(1)} %all-to-all-done.1.refs_0_, bf16[4096,64]{1,0:T(8,128)(2,1)S(1)} %get-tuple-element.28.refs_1_, bf16[40,4096]{1,0:T(8,128)(2,1)S(1)} %get-tuple-element.29.refs_2_, bf16[16,4096]{1,0:T(8,128)(2,1)S(1)} %get-tuple-element.30.refs_3_), custom_call_target="tpu_custom_call" | custom-call | flops 10737418240 | bytes 1048576 | tf_op jit(solution)/shard_map/pallas_call | solution.py:276
  55.0 3.7 %all-to-all-start.2 = ((bf16[16,32,128]{2,1,0:T(8,128)(2,1)}), bf16[16,32,128]{2,1,0:T(8,128)(2,1)S(1)}, u32[]{:S(2)}, u32[]{:S(2)}) async-start(bf16[16,32,128]{2,1,0:T(8,128)(2,1)} %get-tuple-element.31), calls=%async_computation.2 | async-start | bytes 262144 | tf_op jit(solution)/shard_map/all_to_all | solution.py:217
  58.7 4.7 %shard_map.87 = (f32[16,48,128]{2,1,0:T(8,128)S(1)}, bf16[1280,64]{1,0:T(8,128)(2,1)S(1)}, bf16[40,1280]{1,0:T(8,128)(2,1)S(1)}, bf16[16,1280]{1,0:T(8,128)(2,1)S(1)}) custom-call(f32[16,128]{1,0:T(8,128)S(1)} %get-tuple-element.32.refs_0_, f32[48,1280]{1,0:T(8,128)S(1)} %get-tuple-element.35.refs_1_, ...), custom_call_target="tpu_custom_call" | custom-call | flops 5368709120 | bytes 1048576 | tf_op jit(solution)/shard_map/pallas_call | solution.py:288
  63.4 1.9 %collective-permute-start.1 = (f32[16,48,128]{2,1,0:T(8,128)S(1)}, f32[16,48,128]{2,1,0:T(8,128)S(1)}, u32[]{:S(2)}, u32[]{:S(2)}) collective-permute-start(f32[16,48,128]{2,1,0:T(8,128)S(1)} %get-tuple-element.41), channel_id=1, source_target_pairs={{0,32},{32,0},{1,33},{33,1},{2,34},{34,2},{3,35},{35,3},{4,36},{36... | collective-permute-start | bytes 1179656 | tf_op jit(solution)/shard_map/ppermute | solution.py:221
  65.3 4.6 %shard_map.88.a_ref = f32[16,48,128]{2,1,0:T(8,128)S(1)} custom-call(f32[16,128]{1,0:T(8,128)S(1)} %get-tuple-element.32.refs_0_, bf16[16,48,128]{2,1,0:T(8,128)(2,1)S(1)} %all_to_all.20.refs_0_.refs_1_, bf16[64,2048]{1,0:T(8,128)(2,1)S(1)} %get-tuple-element.33.refs_2_, bf16[64,2048]{1,0:T(8,128)(2,1)S(1)} %get-tuple-element.34.refs_3_, ...), custom_call_target="tpu_custom_call" | custom-call | flops 5368709120 | bytes 1048576 | tf_op jit(solution)/shard_map/pallas_call | solution.py:300
  69.9 0.0 collective-permute-done.1.b_ref
  69.9 2.4 %all-to-all-done.2.src_parts_ref = bf16[16,32,128]{2,1,0:T(8,128)(2,1)S(1)} async-done(((bf16[16,32,128]{2,1,0:T(8,128)(2,1)}), bf16[16,32,128]{2,1,0:T(8,128)(2,1)S(1)}, u32[]{:S(2)}, u32[]{:S(2)}) %all-to-all-start.2) | async-done | bytes 131104 | tf_op jit(solution)/shard_map/all_to_all | solution.py:217
  72.4 11.3 %all_to_all.21.tgt_parts_ref = bf16[16,48,128]{2,1,0:T(8,128)(2,1)S(1)} all-to-all(bf16[16,48,128]{2,1,0:T(8,128)(2,1)S(1)} %shard_map.89), channel_id=1, replica_groups=mesh['zl'=8,'core'=2,'zh'=2,'y'=4,'x'=4] {'y','x'}, dimensions={0} | all-to-all | bytes 393216 | tf_op jit(solution)/shard_map/all_to_all | solution.py:217
  83.7 0.7 shard_map.90
  (1 shorter events, 0.0 us)
Async XLA Ops:
  17.6 28.0 %all-to-all-start.1 = ((bf16[16,32,128]{2,1,0:T(8,128)(2,1)}), bf16[16,32,128]{2,1,0:T(8,128)(2,1)S(1)}, u32[]{:S(2)}, u32[]{:S(2)}) async-start(bf16[16,32,128]{2,1,0:T(8,128)(2,1)} %get-tuple-element.26), calls=%async_computation.1 | async-start | bytes 262144 | tf_op jit(solution)/shard_map/all_to_all | solution.py:217
  31.7 3.3 %collective-permute-start = (bf16[16,48,128]{2,1,0:T(8,128)(2,1)S(1)}, bf16[16,48,128]{2,1,0:T(8,128)(2,1)S(1)}, u32[]{:S(2)}, u32[]{:S(2)}) collective-permute-start(bf16[16,48,128]{2,1,0:T(8,128)(2,1)S(1)} %all_to_all.20.refs_0_.refs_1_), channel_id=1, source_target_pairs={{0,32},{32,0},{1,33},{33,1},{2,34},{34,2},{3,35},{35,3},{4,36},{36... | collective-permute-start | bytes 589832 | tf_op jit(solution)/shard_map/ppermute | solution.py:221
  55.0 17.4 %all-to-all-start.2 = ((bf16[16,32,128]{2,1,0:T(8,128)(2,1)}), bf16[16,32,128]{2,1,0:T(8,128)(2,1)S(1)}, u32[]{:S(2)}, u32[]{:S(2)}) async-start(bf16[16,32,128]{2,1,0:T(8,128)(2,1)} %get-tuple-element.31), calls=%async_computation.2 | async-start | bytes 262144 | tf_op jit(solution)/shard_map/all_to_all | solution.py:217
  63.4 6.5 %collective-permute-start.1 = (f32[16,48,128]{2,1,0:T(8,128)S(1)}, f32[16,48,128]{2,1,0:T(8,128)S(1)}, u32[]{:S(2)}, u32[]{:S(2)}) collective-permute-start(f32[16,48,128]{2,1,0:T(8,128)S(1)} %get-tuple-element.41), channel_id=1, source_target_pairs={{0,32},{32,0},{1,33},{33,1},{2,34},{34,2},{3,35},{35,3},{4,36},{36... | collective-permute-start | bytes 1179656 | tf_op jit(solution)/shard_map/ppermute | solution.py:221

commit v8 on v7

--- a/solution.py
+++ b/solution.py
@@ -42,7 +42,7 @@
     return block[:, :width], jnp.concatenate([halves[:rank], halves[rank:]], 1)
 
 
-def copies_kernel(rank_hbm, tgt_hbm, tgt_factor_hbm, src_hbm, src_factor_hbm, tgt_out, src_out, inverse_ref, rank_ref, tgt_ref, tgt_factor_ref, src_ref, src_factor_ref, sems):
+def copies_kernel(rank_hbm, tgt_hbm, tgt_factor_hbm, src_hbm, src_factor_hbm, tgt_out, src_out, inverse_ref, rank_ref, tgt_ref, tgt_factor_ref, src_ref, src_factor_ref, src_copies, sems, out_sem):
     pairs = [
         (rank_hbm, rank_ref),
         (tgt_hbm, tgt_ref),
@@ -53,7 +53,14 @@
     loads = [pltpu.make_async_copy(a, b, sems.at[k]) for k, (a, b) in enumerate(pairs)]
     for load in loads:
         load.start()
-    for load in loads:
+    for load in loads[3:]:
+        load.wait()
+    src_block = pack(src_ref[...].astype(F32), src_factor_ref[...].astype(F32)).astype(BF16)
+    for member in range(src_copies.shape[0]):
+        src_copies[member] = src_block
+    store = pltpu.make_async_copy(src_copies, src_out, out_sem)
+    store.start()
+    for load in loads[:3]:
         load.wait()
     factor = tgt_factor_ref[...]
     inverse_g = inverse_column(rank_ref, factor.shape[1])
@@ -62,9 +69,7 @@
     tgt_block = jnp.concatenate([tgt_ref[...], scaled], 0)
     for member in range(tgt_out.shape[0]):
         tgt_out[member] = tgt_block
-    src_block = pack(src_ref[...].astype(F32), src_factor_ref[...].astype(F32)).astype(BF16)
-    for member in range(src_out.shape[0]):
-        src_out[member] = src_block
+    store.wait()
 
 
 def three_parts(value):
@@ -134,7 +139,7 @@
             bd_ref[:, lanes], bp_ref[:, lanes] = lane_operands(block[:features], block[features:])
 
 
-def source_pair_kernel(scale, width, src_ref, a_ref, gw_ref, gc_ref, out_ref, all_ref, bd_ref, bp_ref, sum_ref):
+def source_pair_kernel(scale, width, src_ref, a_ref, gw_ref, gc_ref, out_hbm, all_ref, bd_ref, bp_ref, out_ref, sems):
     count, features, _ = src_ref.shape
     rank = gc_ref.shape[0]
     for b in range(count):
@@ -145,14 +150,21 @@
     gc = gc_ref[...]
     total = all_ref.shape[1]
     step = total // 2
-    for start in range(0, total, step):
-        at = slice(start, start + step)
+    group = count // 2
+    stores = []
+    for half in range(2):
+        at = slice(half * step, (half + 1) * step)
         sum_w, sum_c = pair_sums(a_ref, gw, gc, bd_ref[:, at], bp_ref[:, at], 1024)
-        sum_ref[:features, at] = feature_gradient(all_ref[:features, at], sum_w, scale)
-        sum_ref[features:, at] = sum_c * scale
-    for b in range(count):
-        block = sum_ref[:, b * width : (b + 1) * width]
-        out_ref[b] = pack(block[:features], block[features:]).astype(out_ref.dtype)
+        feats = feature_gradient(all_ref[:features, at], sum_w, scale)
+        factor = sum_c * scale
+        for b in range(group):
+            lanes = slice(b * width, (b + 1) * width)
+            out_ref[half * group + b] = pack(feats[:, lanes], factor[:, lanes]).astype(out_ref.dtype)
+        part = pl.ds(half * group, group)
+        stores.append(pltpu.make_async_copy(out_ref.at[part], out_hbm.at[part], sems.at[half]))
+        stores[-1].start()
+    for store in stores:
+        store.wait()
 
 
 def target_chunks(scale, inverse_ref, from_ref, a_ref, gw, gc, bd_ref, bp_ref, to_ref):
@@ -196,13 +208,13 @@
     tgt_factor[...] = total[-rank:]
 
 
-def call(kernel, specs, outs, scratch=(), flops=0):
+def call(kernel, specs, outs, scratch=(), flops=0, out_specs=None):
     single = not isinstance(outs, tuple)
     return pl.pallas_call(
         kernel,
         out_shape=outs,
         in_specs=specs,
-        out_specs=VMEM if single else tuple(VMEM for _ in outs),
+        out_specs=out_specs or (VMEM if single else tuple(VMEM for _ in outs)),
         scratch_shapes=scratch,
         compiler_params=pltpu.CompilerParams(vmem_limit_bytes=40 << 20),
         cost_estimate=pl.CostEstimate(flops=flops, transcendentals=0, bytes_accessed=1 << 20),
@@ -246,8 +258,11 @@
             pltpu.VMEM((rank, tgt_width), BF16),
             pltpu.VMEM((features, src_width), BF16),
             pltpu.VMEM((rank, src_width), BF16),
+            pltpu.VMEM((ring, features, LANES), BF16),
             pltpu.SemaphoreType.DMA((5,)),
-        ),
+            pltpu.SemaphoreType.DMA,
+        ),
+        out_specs=(VMEM, HBM, VMEM),
     )(
         *(
             pltpu.with_memory_space_constraint(array, pltpu.HBM)
@@ -280,9 +295,11 @@
         (
             pltpu.VMEM((64, sources), BF16),
             pltpu.VMEM((64, sources), BF16),
-            pltpu.VMEM((rows, sources), F32),
+            pltpu.VMEM((ring, features, LANES), BF16),
+            pltpu.SemaphoreType.DMA((2,)),
         ),
         flops,
+        (HBM, VMEM),
     )(src_blocks, a, gw, gc)
     src_sums = exchange(src_parts, RING)
     send, src_a, src_gw, src_gc = call(

time: 84.9 us -> 84.9 us (level)
  no operation moved by 1% of the time
where the time goes in v8:
time: 84.9 us; the launch traced here: 84.4 us
  blocking collectives  26.7 us (31%)
  starting transfers between devices  21.6 us (25%)
  Pallas kernels  21.5 us (25%)
  waiting for transfers between devices  14 us (16%)
    all_to_all x2, blocking collectives, exchange(): return lax.all_to_all(blocks, axes, 0, 0, tiled=True)  26.7 us
    all_to_all x2, starting transfers between devices, exchange(): return lax.all_to_all(blocks, axes, 0, 0, tiled=True)  17.8 us
    all_to_all x2, waiting for transfers between devices, exchange(): return lax.all_to_all(blocks, axes, 0, 0, tiled=True)  12.6 us
    pallas_call x1, Pallas kernels, local(): call(lambda *refs: source_pair_kernel(scale, src_width, *refs), (VMEM,) *...  9.35 us
    pallas_call x1, Pallas kernels, local(): call(lambda *refs: first_target_kernel(scale, features, *refs), (VMEM,) *...  4.73 us
    pallas_call x1, Pallas kernels, local(): call(lambda *refs: second_target_kernel(scale, *refs), (VMEM,) * 7, shape...  4.56 us
    ppermute x2, starting transfers between devices, swap(): return lax.ppermute(blocks, CORE, [(0, 1), (1, 0)])  3.84 us
  transfers between devices with their start and end apart: 4, of which 3 were waited for; matrix products, arithmetic and copies ran while one was open for 0% of the time, Pallas kernels for 12%

profile of v8, /device:TPU:2, one launch (start us, length us, event | category | flops | bytes accessed | tf_op | source)
XLA Modules:
  0.0 84.4 jit_solution(8502820799583162812)
XLA Ops:
  0.6 1.6 %shard_map.84 = (bf16[16,48,128]{2,1,0:T(8,128)(2,1)S(1)}, bf16[16,32,128]{2,1,0:T(8,128)(2,1)}, f32[16,128]{1,0:T(8,128)S(1)}) custom-call(f32[16]{0:T(128)} %rank_hbm.1, bf16[32,128]{1,0:T(8,128)(2,1)} %tgt_hbm.1, bf16[16,128]{1,0:T(8,128)(2,1)} %tgt_factor_hbm.1, bf16[32,80]{1,0:T(8,128)(2,1)} %src_hbm.1, bf16[16,80]{1,0:T(8,128)(2,1)} %src_factor_hbm.1), custom_call_target="tpu_custom_call" | custom-call | bytes 1048576 | tf_op jit(solution)/shard_map/pallas_call | solution.py:247
  2.2 15.4 %all_to_all.20.refs_0_.refs_1_ = bf16[16,48,128]{2,1,0:T(8,128)(2,1)S(1)} all-to-all(bf16[16,48,128]{2,1,0:T(8,128)(2,1)S(1)} %get-tuple-element.24), channel_id=1, replica_groups=mesh['zl'=8,'core'=2,'zh'=2,'y'=4,'x'=4] {'y','x'}, dimensions={0} | all-to-all | bytes 393216 | tf_op jit(solution)/shard_map/all_to_all | solution.py:229
  17.6 14.1 %all-to-all-start.1 = ((bf16[16,32,128]{2,1,0:T(8,128)(2,1)}), bf16[16,32,128]{2,1,0:T(8,128)(2,1)S(1)}, u32[]{:S(2)}, u32[]{:S(2)}) async-start(bf16[16,32,128]{2,1,0:T(8,128)(2,1)} %get-tuple-element.26), calls=%async_computation.1 | async-start | bytes 262144 | tf_op jit(solution)/shard_map/all_to_all | solution.py:229
  31.7 1.9 %collective-permute-start = (bf16[16,48,128]{2,1,0:T(8,128)(2,1)S(1)}, bf16[16,48,128]{2,1,0:T(8,128)(2,1)S(1)}, u32[]{:S(2)}, u32[]{:S(2)}) collective-permute-start(bf16[16,48,128]{2,1,0:T(8,128)(2,1)S(1)} %all_to_all.20.refs_0_.refs_1_), channel_id=1, source_target_pairs={{0,32},{32,0},{1,33},{33,1},{2,34},{34,2},{3,35},{35,3},{4,36},{36... | collective-permute-start | bytes 589832 | tf_op jit(solution)/shard_map/ppermute | solution.py:233
  33.6 1.4 %collective-permute-done.refs_1_.refs_2_ = bf16[16,48,128]{2,1,0:T(8,128)(2,1)S(1)} collective-permute-done((bf16[16,48,128]{2,1,0:T(8,128)(2,1)S(1)}, bf16[16,48,128]{2,1,0:T(8,128)(2,1)S(1)}, u32[]{:S(2)}, u32[]{:S(2)}) %collective-permute-start) | collective-permute-done | bytes 196640 | tf_op jit(solution)/shard_map/ppermute | solution.py:233
  35.0 0.5 shard_map.85
  35.5 10.1 %all-to-all-done.1.refs_0_ = bf16[16,32,128]{2,1,0:T(8,128)(2,1)S(1)} async-done(((bf16[16,32,128]{2,1,0:T(8,128)(2,1)}), bf16[16,32,128]{2,1,0:T(8,128)(2,1)S(1)}, u32[]{:S(2)}, u32[]{:S(2)}) %all-to-all-start.1) | async-done | bytes 131104 | tf_op jit(solution)/shard_map/all_to_all | solution.py:229
  45.6 9.4 %shard_map.86 = (bf16[16,32,128]{2,1,0:T(8,128)(2,1)}, f32[48,1280]{1,0:T(8,128)S(1)}) custom-call(bf16[16,32,128]{2,1,0:T(8,128)(2,1)S(1)} %all-to-all-done.1.refs_0_, bf16[4096,64]{1,0:T(8,128)(2,1)S(1)} %get-tuple-element.28.refs_1_, bf16[40,4096]{1,0:T(8,128)(2,1)S(1)} %get-tuple-element.29.refs_2_, bf16[16,4096]{1,0:T(8,128)(2,1)S(1)} %get-tuple-element.30.refs_3_), custom_call_target="tpu_custom_call" | custom-call | flops 10737418240 | bytes 1048576 | tf_op jit(solution)/shard_map/pallas_call | solution.py:291
  55.0 3.7 %all-to-all-start.2 = ((bf16[16,32,128]{2,1,0:T(8,128)(2,1)}), bf16[16,32,128]{2,1,0:T(8,128)(2,1)S(1)}, u32[]{:S(2)}, u32[]{:S(2)}) async-start(bf16[16,32,128]{2,1,0:T(8,128)(2,1)} %get-tuple-element.31), calls=%async_computation.2 | async-start | bytes 262144 | tf_op jit(solution)/shard_map/all_to_all | solution.py:229
  58.7 4.7 %shard_map.87 = (f32[16,48,128]{2,1,0:T(8,128)S(1)}, bf16[1280,64]{1,0:T(8,128)(2,1)S(1)}, bf16[40,1280]{1,0:T(8,128)(2,1)S(1)}, bf16[16,1280]{1,0:T(8,128)(2,1)S(1)}) custom-call(f32[16,128]{1,0:T(8,128)S(1)} %get-tuple-element.32.refs_0_, f32[48,1280]{1,0:T(8,128)S(1)} %get-tuple-element.35.refs_1_, ...), custom_call_target="tpu_custom_call" | custom-call | flops 5368709120 | bytes 1048576 | tf_op jit(solution)/shard_map/pallas_call | solution.py:305
  63.4 1.9 %collective-permute-start.1 = (f32[16,48,128]{2,1,0:T(8,128)S(1)}, f32[16,48,128]{2,1,0:T(8,128)S(1)}, u32[]{:S(2)}, u32[]{:S(2)}) collective-permute-start(f32[16,48,128]{2,1,0:T(8,128)S(1)} %get-tuple-element.41), channel_id=1, source_target_pairs={{0,32},{32,0},{1,33},{33,1},{2,34},{34,2},{3,35},{35,3},{4,36},{36... | collective-permute-start | bytes 1179656 | tf_op jit(solution)/shard_map/ppermute | solution.py:233
  65.4 4.6 %shard_map.88.a_ref = f32[16,48,128]{2,1,0:T(8,128)S(1)} custom-call(f32[16,128]{1,0:T(8,128)S(1)} %get-tuple-element.32.refs_0_, bf16[16,48,128]{2,1,0:T(8,128)(2,1)S(1)} %all_to_all.20.refs_0_.refs_1_, bf16[64,2048]{1,0:T(8,128)(2,1)S(1)} %get-tuple-element.33.refs_2_, bf16[64,2048]{1,0:T(8,128)(2,1)S(1)} %get-tuple-element.34.refs_3_, ...), custom_call_target="tpu_custom_call" | custom-call | flops 5368709120 | bytes 1048576 | tf_op jit(solution)/shard_map/pallas_call | solution.py:317
  69.9 0.0 collective-permute-done.1.b_ref
  70.0 2.4 %all-to-all-done.2.src_parts_ref = bf16[16,32,128]{2,1,0:T(8,128)(2,1)S(1)} async-done(((bf16[16,32,128]{2,1,0:T(8,128)(2,1)}), bf16[16,32,128]{2,1,0:T(8,128)(2,1)S(1)}, u32[]{:S(2)}, u32[]{:S(2)}) %all-to-all-start.2) | async-done | bytes 131104 | tf_op jit(solution)/shard_map/all_to_all | solution.py:229
  72.4 11.3 %all_to_all.21.tgt_parts_ref = bf16[16,48,128]{2,1,0:T(8,128)(2,1)S(1)} all-to-all(bf16[16,48,128]{2,1,0:T(8,128)(2,1)S(1)} %shard_map.89), channel_id=1, replica_groups=mesh['zl'=8,'core'=2,'zh'=2,'y'=4,'x'=4] {'y','x'}, dimensions={0} | all-to-all | bytes 393216 | tf_op jit(solution)/shard_map/all_to_all | solution.py:229
  83.7 0.7 shard_map.90
  (1 shorter events, 0.0 us)
Async XLA Ops:
  17.6 28.0 %all-to-all-start.1 = ((bf16[16,32,128]{2,1,0:T(8,128)(2,1)}), bf16[16,32,128]{2,1,0:T(8,128)(2,1)S(1)}, u32[]{:S(2)}, u32[]{:S(2)}) async-start(bf16[16,32,128]{2,1,0:T(8,128)(2,1)} %get-tuple-element.26), calls=%async_computation.1 | async-start | bytes 262144 | tf_op jit(solution)/shard_map/all_to_all | solution.py:229
  31.7 3.3 %collective-permute-start = (bf16[16,48,128]{2,1,0:T(8,128)(2,1)S(1)}, bf16[16,48,128]{2,1,0:T(8,128)(2,1)S(1)}, u32[]{:S(2)}, u32[]{:S(2)}) collective-permute-start(bf16[16,48,128]{2,1,0:T(8,128)(2,1)S(1)} %all_to_all.20.refs_0_.refs_1_), channel_id=1, source_target_pairs={{0,32},{32,0},{1,33},{33,1},{2,34},{34,2},{3,35},{35,3},{4,36},{36... | collective-permute-start | bytes 589832 | tf_op jit(solution)/shard_map/ppermute | solution.py:233
  55.0 17.4 %all-to-all-start.2 = ((bf16[16,32,128]{2,1,0:T(8,128)(2,1)}), bf16[16,32,128]{2,1,0:T(8,128)(2,1)S(1)}, u32[]{:S(2)}, u32[]{:S(2)}) async-start(bf16[16,32,128]{2,1,0:T(8,128)(2,1)} %get-tuple-element.31), calls=%async_computation.2 | async-start | bytes 262144 | tf_op jit(solution)/shard_map/all_to_all | solution.py:229
  63.4 6.5 %collective-permute-start.1 = (f32[16,48,128]{2,1,0:T(8,128)S(1)}, f32[16,48,128]{2,1,0:T(8,128)S(1)}, u32[]{:S(2)}, u32[]{:S(2)}) collective-permute-start(f32[16,48,128]{2,1,0:T(8,128)S(1)} %get-tuple-element.41), channel_id=1, source_target_pairs={{0,32},{32,0},{1,33},{33,1},{2,34},{34,2},{3,35},{35,3},{4,36},{36... | collective-permute-start | bytes 1179656 | tf_op jit(solution)/shard_map/ppermute | solution.py:233

commit v9 on v7

--- a/solution.py
+++ b/solution.py
@@ -6,7 +6,7 @@
 from jax.sharding import Mesh
 from jax.sharding import PartitionSpec as P
 
-RING = ("zh", "zl")
+RING = ("zl", "zh")
 PLANE = ("y", "x")
 CORE = "core"
 BF16 = jnp.bfloat16

time: 84.9 us -> 86.2 us (1.015)
  the two profiles are of different devices: /device:TPU:2 before, /device:TPU:32 now
where the time goes in v9:
time: 86.2 us; the launch traced here: 85.7 us
  blocking collectives  26.6 us (31%)
  starting transfers between devices  23.1 us (27%)
  Pallas kernels  21.4 us (25%)
  waiting for transfers between devices  14 us (16%)
    all_to_all x2, blocking collectives, exchange(): return lax.all_to_all(blocks, axes, 0, 0, tiled=True)  26.6 us
    all_to_all x2, starting transfers between devices, exchange(): return lax.all_to_all(blocks, axes, 0, 0, tiled=True)  19.2 us
    all_to_all x2, waiting for transfers between devices, exchange(): return lax.all_to_all(blocks, axes, 0, 0, tiled=True)  12.6 us
    pallas_call x1, Pallas kernels, local(): call(lambda *refs: source_pair_kernel(scale, src_width, *refs), (VMEM,) *...  9.34 us
    pallas_call x1, Pallas kernels, local(): call(lambda *refs: first_target_kernel(scale, features, *refs), (VMEM,) *...  4.73 us
    pallas_call x1, Pallas kernels, local(): call(lambda *refs: second_target_kernel(scale, *refs), (VMEM,) * 7, shape...  4.56 us
    ppermute x2, starting transfers between devices, swap(): return lax.ppermute(blocks, CORE, [(0, 1), (1, 0)])  3.83 us
  transfers between devices with their start and end apart: 4, of which 3 were waited for; matrix products, arithmetic and copies ran while one was open for 0% of the time, Pallas kernels for 11%

profile of v9, /device:TPU:32, one launch (start us, length us, event | category | flops | bytes accessed | tf_op | source)
XLA Modules:
  0.0 85.7 jit_solution(6570599851096686704)
XLA Ops:
  0.6 1.6 %shard_map.84 = (bf16[16,48,128]{2,1,0:T(8,128)(2,1)S(1)}, bf16[16,32,128]{2,1,0:T(8,128)(2,1)}, f32[16,128]{1,0:T(8,128)S(1)}) custom-call(f32[16]{0:T(128)} %rank_hbm.1, bf16[32,128]{1,0:T(8,128)(2,1)} %tgt_hbm.1, bf16[16,128]{1,0:T(8,128)(2,1)} %tgt_factor_hbm.1, bf16[32,80]{1,0:T(8,128)(2,1)} %src_hbm.1, bf16[16,80]{1,0:T(8,128)(2,1)} %src_factor_hbm.1), custom_call_target="tpu_custom_call" | custom-call | bytes 1048576 | tf_op jit(solution)/shard_map/pallas_call | solution.py:235
  2.2 15.2 %all_to_all.20.refs_0_.refs_1_ = bf16[16,48,128]{2,1,0:T(8,128)(2,1)S(1)} all-to-all(bf16[16,48,128]{2,1,0:T(8,128)(2,1)S(1)} %get-tuple-element.24), channel_id=1, replica_groups=mesh['zl'=8,'core'=2,'zh'=2,'y'=4,'x'=4] {'y','x'}, dimensions={0} | all-to-all | bytes 393216 | tf_op jit(solution)/shard_map/all_to_all | solution.py:217
  17.4 15.2 %all-to-all-start.1 = ((bf16[16,32,128]{2,1,0:T(8,128)(2,1)}), bf16[16,32,128]{2,1,0:T(8,128)(2,1)S(1)}, u32[]{:S(2)}, u32[]{:S(2)}) async-start(bf16[16,32,128]{2,1,0:T(8,128)(2,1)} %get-tuple-element.26), calls=%async_computation.1 | async-start | bytes 262144 | tf_op jit(solution)/shard_map/all_to_all | solution.py:217
  32.6 1.9 %collective-permute-start = (bf16[16,48,128]{2,1,0:T(8,128)(2,1)S(1)}, bf16[16,48,128]{2,1,0:T(8,128)(2,1)S(1)}, u32[]{:S(2)}, u32[]{:S(2)}) collective-permute-start(bf16[16,48,128]{2,1,0:T(8,128)(2,1)S(1)} %all_to_all.20.refs_0_.refs_1_), channel_id=1, source_target_pairs={{0,32},{32,0},{1,33},{33,1},{2,34},{34,2},{3,35},{35,3},{4,36},{36... | collective-permute-start | bytes 589832 | tf_op jit(solution)/shard_map/ppermute | solution.py:221
  34.5 1.4 %collective-permute-done.refs_1_.refs_2_ = bf16[16,48,128]{2,1,0:T(8,128)(2,1)S(1)} collective-permute-done((bf16[16,48,128]{2,1,0:T(8,128)(2,1)S(1)}, bf16[16,48,128]{2,1,0:T(8,128)(2,1)S(1)}, u32[]{:S(2)}, u32[]{:S(2)}) %collective-permute-start) | collective-permute-done | bytes 196640 | tf_op jit(solution)/shard_map/ppermute | solution.py:221
  35.9 0.5 shard_map.85
  36.4 10.0 %all-to-all-done.1.refs_0_ = bf16[16,32,128]{2,1,0:T(8,128)(2,1)S(1)} async-done(((bf16[16,32,128]{2,1,0:T(8,128)(2,1)}), bf16[16,32,128]{2,1,0:T(8,128)(2,1)S(1)}, u32[]{:S(2)}, u32[]{:S(2)}) %all-to-all-start.1) | async-done | bytes 131104 | tf_op jit(solution)/shard_map/all_to_all | solution.py:217
  46.4 9.3 %shard_map.86 = (bf16[16,32,128]{2,1,0:T(8,128)(2,1)}, f32[48,1280]{1,0:T(8,128)S(1)}) custom-call(bf16[16,32,128]{2,1,0:T(8,128)(2,1)S(1)} %all-to-all-done.1.refs_0_, bf16[4096,64]{1,0:T(8,128)(2,1)S(1)} %get-tuple-element.28.refs_1_, bf16[40,4096]{1,0:T(8,128)(2,1)S(1)} %get-tuple-element.29.refs_2_, bf16[16,4096]{1,0:T(8,128)(2,1)S(1)} %get-tuple-element.30.refs_3_), custom_call_target="tpu_custom_call" | custom-call | flops 10737418240 | bytes 1048576 | tf_op jit(solution)/shard_map/pallas_call | solution.py:276
  55.8 4.0 %all-to-all-start.2 = ((bf16[16,32,128]{2,1,0:T(8,128)(2,1)}), bf16[16,32,128]{2,1,0:T(8,128)(2,1)S(1)}, u32[]{:S(2)}, u32[]{:S(2)}) async-start(bf16[16,32,128]{2,1,0:T(8,128)(2,1)} %get-tuple-element.31), calls=%async_computation.2 | async-start | bytes 262144 | tf_op jit(solution)/shard_map/all_to_all | solution.py:217
  59.8 4.7 %shard_map.87 = (f32[16,48,128]{2,1,0:T(8,128)S(1)}, bf16[1280,64]{1,0:T(8,128)(2,1)S(1)}, bf16[40,1280]{1,0:T(8,128)(2,1)S(1)}, bf16[16,1280]{1,0:T(8,128)(2,1)S(1)}) custom-call(f32[16,128]{1,0:T(8,128)S(1)} %get-tuple-element.32.refs_0_, f32[48,1280]{1,0:T(8,128)S(1)} %get-tuple-element.35.refs_1_, ...), custom_call_target="tpu_custom_call" | custom-call | flops 5368709120 | bytes 1048576 | tf_op jit(solution)/shard_map/pallas_call | solution.py:288
  64.5 1.9 %collective-permute-start.1 = (f32[16,48,128]{2,1,0:T(8,128)S(1)}, f32[16,48,128]{2,1,0:T(8,128)S(1)}, u32[]{:S(2)}, u32[]{:S(2)}) collective-permute-start(f32[16,48,128]{2,1,0:T(8,128)S(1)} %get-tuple-element.41), channel_id=1, source_target_pairs={{0,32},{32,0},{1,33},{33,1},{2,34},{34,2},{3,35},{35,3},{4,36},{36... | collective-permute-start | bytes 1179656 | tf_op jit(solution)/shard_map/ppermute | solution.py:221
  66.4 4.6 %shard_map.88.a_ref = f32[16,48,128]{2,1,0:T(8,128)S(1)} custom-call(f32[16,128]{1,0:T(8,128)S(1)} %get-tuple-element.32.refs_0_, bf16[16,48,128]{2,1,0:T(8,128)(2,1)S(1)} %all_to_all.20.refs_0_.refs_1_, bf16[64,2048]{1,0:T(8,128)(2,1)S(1)} %get-tuple-element.33.refs_2_, bf16[64,2048]{1,0:T(8,128)(2,1)S(1)} %get-tuple-element.34.refs_3_, ...), custom_call_target="tpu_custom_call" | custom-call | flops 5368709120 | bytes 1048576 | tf_op jit(solution)/shard_map/pallas_call | solution.py:300
  71.0 0.0 collective-permute-done.1.b_ref
  71.1 2.6 %all-to-all-done.2.src_parts_ref = bf16[16,32,128]{2,1,0:T(8,128)(2,1)S(1)} async-done(((bf16[16,32,128]{2,1,0:T(8,128)(2,1)}), bf16[16,32,128]{2,1,0:T(8,128)(2,1)S(1)}, u32[]{:S(2)}, u32[]{:S(2)}) %all-to-all-start.2) | async-done | bytes 131104 | tf_op jit(solution)/shard_map/all_to_all | solution.py:217
  73.6 11.4 %all_to_all.21.tgt_parts_ref = bf16[16,48,128]{2,1,0:T(8,128)(2,1)S(1)} all-to-all(bf16[16,48,128]{2,1,0:T(8,128)(2,1)S(1)} %shard_map.89), channel_id=1, replica_groups=mesh['zl'=8,'core'=2,'zh'=2,'y'=4,'x'=4] {'y','x'}, dimensions={0} | all-to-all | bytes 393216 | tf_op jit(solution)/shard_map/all_to_all | solution.py:217
  85.0 0.7 shard_map.90
  (1 shorter events, 0.0 us)
Async XLA Ops:
  17.4 29.0 %all-to-all-start.1 = ((bf16[16,32,128]{2,1,0:T(8,128)(2,1)}), bf16[16,32,128]{2,1,0:T(8,128)(2,1)S(1)}, u32[]{:S(2)}, u32[]{:S(2)}) async-start(bf16[16,32,128]{2,1,0:T(8,128)(2,1)} %get-tuple-element.26), calls=%async_computation.1 | async-start | bytes 262144 | tf_op jit(solution)/shard_map/all_to_all | solution.py:217
  32.6 3.3 %collective-permute-start = (bf16[16,48,128]{2,1,0:T(8,128)(2,1)S(1)}, bf16[16,48,128]{2,1,0:T(8,128)(2,1)S(1)}, u32[]{:S(2)}, u32[]{:S(2)}) collective-permute-start(bf16[16,48,128]{2,1,0:T(8,128)(2,1)S(1)} %all_to_all.20.refs_0_.refs_1_), channel_id=1, source_target_pairs={{0,32},{32,0},{1,33},{33,1},{2,34},{34,2},{3,35},{35,3},{4,36},{36... | collective-permute-start | bytes 589832 | tf_op jit(solution)/shard_map/ppermute | solution.py:221
  55.8 17.9 %all-to-all-start.2 = ((bf16[16,32,128]{2,1,0:T(8,128)(2,1)}), bf16[16,32,128]{2,1,0:T(8,128)(2,1)S(1)}, u32[]{:S(2)}, u32[]{:S(2)}) async-start(bf16[16,32,128]{2,1,0:T(8,128)(2,1)} %get-tuple-element.31), calls=%async_computation.2 | async-start | bytes 262144 | tf_op jit(solution)/shard_map/all_to_all | solution.py:217
  64.5 6.5 %collective-permute-start.1 = (f32[16,48,128]{2,1,0:T(8,128)S(1)}, f32[16,48,128]{2,1,0:T(8,128)S(1)}, u32[]{:S(2)}, u32[]{:S(2)}) collective-permute-start(f32[16,48,128]{2,1,0:T(8,128)S(1)} %get-tuple-element.41), channel_id=1, source_target_pairs={{0,32},{32,0},{1,33},{33,1},{2,34},{34,2},{3,35},{35,3},{4,36},{36... | collective-permute-start | bytes 1179656 | tf_op jit(solution)/shard_map/ppermute | solution.py:221
